TPU v7x, 128 devices: a whole 4x4x4 slice. The times are simulated.
128 devices in a mesh: gx: 16 (over x, y), gy: 8 (over z, core).
Axes of the slice: x: 4, y: 4, z: 4, core: 2. Of those that a mesh axis runs over, the one named last changes fastest.
Arguments:
- log_density: float32 [512, 512, 512], P('gx', 'gy'), may hold values from -3 to 3
- weights: bfloat16 [8192, 32, 32, 128], P(('gx', 'gy')), may hold values from -0.09375 to 0.09375
- observed: float32 [8192, 32], P(('gx', 'gy')), may hold values from -6 to 6
- inverse_var: float32 [8192, 32], P(('gx', 'gy')), may hold values from 0.25 to 4
- star_counts: int32 [8192], P(('gx', 'gy')), may hold values from 1 to 32
- block_ids: int32 [8192, 32], P(('gx', 'gy')), may hold values from 0 to 1048575, as said below
Outputs:
- new_log_density: float32 [512, 512, 512], P('gx', 'gy')
- extinction: float32 [8192, 32], P(('gx', 'gy'))
Inputs may be any that keep to these rules, and one draw needn't show every extreme that they name: `block_ids`: among the 2048 ids of one device's rows (rows d * 64 to (d + 1) * 64 - 1), at most 32 name blocks of any one tile (blocks t * 8192 to (t + 1) * 8192 - 1), and exactly 32 name blocks of tile d.
All inputs are finite; a program needn't handle non-finite values.
Results may differ from a plain program's by a relative error of at most 0.0029.
Values may be sent and summed in bfloat16 or wider, within the bound.
A program may use at most 128 MiB of HBM per device.

v0:
```python
import jax
import jax.numpy as jnp
from jax import lax
from jax.sharding import PartitionSpec as P

shift_kappa = 0.5
prior_weight = 0.05
step_rate = 2.0


def extended(x, sides, width):
    for axis, dim in sides:
        peers, length = (lax.axis_size(axis), x.shape[dim])
        up = [(i, (i + 1) % peers) for i in range(peers - 1)]
        down = [(j, i) for i, j in up]
        last = lax.slice_in_dim(x, length - width, length, axis=dim)
        first = lax.slice_in_dim(x, 0, width, axis=dim)
        before = lax.ppermute(last, axis, up)
        after = lax.ppermute(first, axis, down)
        x = jnp.concatenate([before, x, after], axis=dim)
    return x


def apply_op(padded):
    center = padded[1:-1, 1:-1, :]
    beside = padded[2:, 1:-1, :] + padded[:-2, 1:-1, :]
    beside = beside + padded[1:-1, 2:, :] + padded[1:-1, :-2, :]
    blank_plane = jnp.zeros(center.shape[:2] + (1,), jnp.float32)
    beside = beside + jnp.concatenate([center[:, :, 1:], blank_plane], 2)
    beside = beside + jnp.concatenate([blank_plane, center[:, :, :-1]], 2)
    return (shift_kappa + 6.0) * center - beside


def on_device(log_density, weights, observed, inverse_var, star_counts, block_ids):
    cells_x, cells_y, depth = log_density.shape
    blocks_dev, slots, stars, width = weights.shape
    size_x = lax.axis_size("gx")
    size_y = lax.axis_size("gy")
    devices = size_x * size_y
    requests = blocks_dev * slots
    capacity = 2 * requests // devices
    local_blocks = cells_x * cells_y * (depth // width)
    flat_ids = block_ids.reshape(requests)
    target = flat_ids // local_blocks
    within = flat_ids % local_blocks
    onehot = (target[:, None] == jnp.arange(devices, dtype=jnp.int32)[None, :]).astype(jnp.int32)
    ranked = jnp.sum(jnp.cumsum(onehot, 0) * onehot, 1) - 1
    position = target * capacity + ranked
    outgoing = jnp.full((devices * capacity,), -1, jnp.int32).at[position].set(within)
    incoming = lax.all_to_all(
        outgoing.reshape(devices, capacity), ("gx", "gy"), split_axis=0, concat_axis=0, tiled=True
    ).reshape(-1)
    dens_field = jnp.exp(log_density)
    table = dens_field.astype(jnp.bfloat16).reshape(local_blocks, width)
    present = incoming >= 0
    served = jnp.where(
        present[:, None], table[jnp.maximum(incoming, 0)], jnp.zeros((), jnp.bfloat16)
    )
    returned = lax.all_to_all(
        served.reshape(devices, capacity, width),
        ("gx", "gy"),
        split_axis=0,
        concat_axis=0,
        tiled=True,
    )
    fetched = returned.reshape(devices * capacity, width)[position].reshape(
        blocks_dev, slots, width
    )
    extinction = jnp.einsum("bksv,bkv->bs", weights, fetched, preferred_element_type=jnp.float32)
    live = jnp.arange(stars)[None, :] < star_counts[:, None]
    weighted = jnp.where(live, inverse_var * (extinction - observed), 0.0).astype(jnp.bfloat16)
    sens = jnp.einsum(
        "bksv,bs->bkv", weights, weighted, preferred_element_type=jnp.float32
    ).reshape(requests, width)
    parcel = jnp.zeros((devices * capacity, width), jnp.float32).at[position].set(sens)
    arrived = lax.all_to_all(
        parcel.reshape(devices, capacity, width),
        ("gx", "gy"),
        split_axis=0,
        concat_axis=0,
        tiled=True,
    )
    arrived = arrived.reshape(devices * capacity, width)
    first_pad = extended(log_density, (("gx", 0), ("gy", 1)), 1)
    smooth = apply_op(first_pad)
    second_pad = extended(smooth, (("gx", 0), ("gy", 1)), 1)
    prior_grad = apply_op(second_pad)
    slot_target = jnp.where(present, incoming, local_blocks)
    collected = (
        jnp.zeros((local_blocks, width), jnp.float32).at[slot_target].add(arrived, mode="drop")
    )
    data_grad = collected.reshape(cells_x, cells_y, depth) * dens_field
    new_log_density = log_density - step_rate * (data_grad + prior_weight * prior_grad)
    return (new_log_density, extinction)


def solution(mesh):
    placed = (
        P("gx", "gy", None),
        P(("gx", "gy"), None, None, None),
        P(("gx", "gy"), None),
        P(("gx", "gy"), None),
        P(("gx", "gy")),
        P(("gx", "gy"), None),
    )
    return jax.shard_map(
        on_device,
        mesh=mesh,
        in_specs=placed,
        out_specs=(P("gx", "gy", None), P(("gx", "gy"), None)),
        check_vma=False,
    )
```

profile of v0, /device:TPU:1, one launch (start us, length us, event | category | flops | bytes accessed | tf_op | source)
XLA Modules:
  0.0 237.0 jit_solution(14565669224113128184)
XLA Ops:
  1.6 4.0 %collective-permute-start.1 = (f32[1,64,512]{2,1,0:T(8,128)S(1)}, f32[1,64,512]{2,1,0:T(8,128)S(1)}, u32[]{:S(2)}, u32[]{:S(2)}) collective-permute-start(f32[1,64,512]{2,1,0:T(8,128)S(1)} %get-tuple-element.17), channel_id=1, source_target_pairs={{0,8},{8,16},{16,24},{24,32},{32,40},{40,48},{48,56},{56,64},{64,7... | collective-permute-start | bytes 393224 | tf_op jit(solution)/shard_map/ppermute | solution.py:18
  5.7 1.3 collective-permute-start
  9.7 8.1 %scatter_custom_fusion = s32[4096]{0:T(1024)S(1)} fusion(s32[2048]{0:T(1024)S(1)} %bitcast.40, s32[2048]{0:T(1024)S(1)} %get-tuple-element.20, s32[]{:T(128)} %constant.27.clone.1), kind=kCustom, calls=%fused_computation.78 | custom fusion | bytes 16388 | tf_op jit(solution)/shard_map/scatter | solution.py:49
  18.4 12.0 %all-to-all-start = ((s32[128,1,32]{2,1,0:T(1,128)}), s32[128,1,32]{2,1,0:T(1,128)S(1)}, u32[]{:S(2)}, u32[]{:S(2)}) async-start(s32[128,1,32]{2,1,0:T(1,128)} %bitcast.5), calls=%async_computation | async-start | bytes 131072 | tf_op jit(solution)/shard_map/all_to_all | solution.py:50
  30.5 8.1 %fusion.36 = (f32[32,64,511]{2,1,0:T(8,128)}, f32[32,64,511]{2,1,0:T(8,128)}) fusion(f32[32,64,512]{2,1,0:T(8,128)} %param.6), kind=kLoop, calls=%fused_computation.91 | loop fusion | bytes 16744448 | tf_op jit(solution)/shard_map/slice | solution.py:29
  38.5 1.3 all-to-all-done
  41.4 2.8 %constant_dynamic-update-slice_fusion.1 = f32[34,64,512]{2,1,0:T(8,128)S(1)} fusion(f32[34,64,512]{2,1,0:T(8,128)S(1)} %constant_dynamic-update-slice_fusion.2, f32[32,64,512]{2,1,0:T(8,128)} %param.6), kind=kLoop, calls=%fused_computation.83 | loop fusion | bytes 8388608
  44.2 2.0 copy-done.1
  46.4 3.1 %collective-permute-start.2 = (f32[34,1,512]{2,0,1:T(8,128)S(1)}, f32[34,1,512]{2,0,1:T(8,128)S(1)}, u32[]{:S(2)}, u32[]{:S(2)}) collective-permute-start(f32[34,1,512]{2,0,1:T(8,128)S(1)} %copy.39), channel_id=1, source_target_pairs={{1,0},{2,1},{3,2},{4,3},{5,4},{6,5},{7,6},{9,8},{10,9},{11,10},{12... | collective-permute-start | bytes 208904 | tf_op jit(solution)/shard_map/ppermute | solution.py:19
  49.5 2.4 %collective-permute-start.3 = (f32[34,1,512]{2,0,1:T(8,128)S(1)}, f32[34,1,512]{2,0,1:T(8,128)S(1)}, u32[]{:S(2)}, u32[]{:S(2)}) collective-permute-start(f32[34,1,512]{2,0,1:T(8,128)S(1)} %copy.41), channel_id=1, source_target_pairs={{0,1},{1,2},{2,3},{3,4},{4,5},{5,6},{6,7},{8,9},{9,10},{10,11},{11... | collective-permute-start | bytes 208904 | tf_op jit(solution)/shard_map/ppermute | solution.py:18
  52.2 1.2 collective-permute-done.3
  53.5 16.6 %exponential_convert_fusion = (bf16[32,64,512]{2,1,0:T(8,128)(2,1)}, f32[32,64,512]{2,1,0:T(8,128)}) fusion(f32[32,64,512]{2,1,0:T(8,128)} %param.6, f32[32,64,511]{2,1,0:T(8,128)} %get-tuple-element.15, f32[32,64,511]{2,1,0:T(8,128)} %get-tuple-element.14, f32[34,64,512]{2,1,0:T(8,128)} %copy-done.1, f32[34,1,512]{2,1,0:T(1,128)S(1)} %copy.42, ...), kind=kLoop, calls=%fused_computation.33 | loop fusion | flops 12582912 | bytes 23715840 | tf_op jit(solution)/shard_map/convert_element_type | solution.py:54
  70.2 3.1 %reshape.221 = bf16[8192,128]{1,0:T(8,128)(2,1)S(1)} reshape(bf16[32,64,512]{2,1,0:T(8,128)(2,1)} %get-tuple-element.8) | data formatting | bytes 4194304 | tf_op jit(solution)/shard_map/reshape | solution.py:54
  73.3 12.1 %gather_fusion = bf16[4096,128]{1,0:T(8,128)(2,1)S(1)} fusion(bf16[8192,128]{1,0:T(8,128)(2,1)S(1)} %reshape.221, s32[4096]{0:T(1024)S(1)} %broadcast_clamp_fusion), kind=kCustom, calls=%fused_computation | custom fusion | bytes 2113536 | tf_op jit(solution)/shard_map/gather | solution.py:57
  85.4 2.0 broadcast_select_fusion
  87.4 9.5 %all-to-all-start.1 = ((bf16[128,32,128]{2,1,0:T(8,128)(2,1)}), bf16[128,32,128]{2,1,0:T(8,128)(2,1)S(1)}, u32[]{:S(2)}, u32[]{:S(2)}) async-start(bf16[128,32,128]{2,1,0:T(8,128)(2,1)} %broadcast_select_fusion), calls=%async_computation.1 | async-start | bytes 2097152 | tf_op jit(solution)/shard_map/all_to_all | solution.py:59
  96.9 19.3 %all-to-all-done.1 = bf16[128,32,128]{2,1,0:T(8,128)(2,1)S(1)} async-done(((bf16[128,32,128]{2,1,0:T(8,128)(2,1)}), bf16[128,32,128]{2,1,0:T(8,128)(2,1)S(1)}, u32[]{:S(2)}, u32[]{:S(2)}) %all-to-all-start.1) | async-done | bytes 1048608 | tf_op jit(solution)/shard_map/all_to_all | solution.py:59
  116.1 6.2 %gather_fusion.1 = bf16[2048,128]{1,0:T(8,128)(2,1)S(1)} fusion(bf16[4096,128]{1,0:T(8,128)(2,1)S(1)} %bitcast.33, s32[2048]{0:T(1024)S(1)} %broadcast_clamp_fusion.1), kind=kCustom, calls=%fused_computation.1 | custom fusion | bytes 1056768 | tf_op jit(solution)/shard_map/gather | solution.py:66
  122.4 8.2 %fusion.19 = f32[64,1,32,1]{2,1,3,0:T(1,128)S(1)} fusion(bf16[64,32,32,128]{3,2,1,0:T(8,128)(2,1)} %param.7, bf16[64,32,128,1]{2,1,0,3:T(8,128)(2,1)S(1)} %bitcast.37), kind=kOutput, calls=%fused_computation.38 | convolution fusion | flops 16777216 | bytes 17309696 | tf_op jit(solution)/shard_map/bksv,bkv->bs/dot_general | solution.py:69
  130.8 8.0 %fusion.38 = f32[64,1,32,128]{3,1,2,0:T(1,128)S(1)} fusion(bf16[64,32,1,1]{1,2,3,0:T(2,128)(2,1)S(1)} %copy.49, bf16[64,32,32,128]{3,2,1,0:T(8,128)(2,1)} %param.7), kind=kOutput, calls=%fused_computation.93 | convolution fusion | flops 16777216 | bytes 17829888 | tf_op jit(solution)/shard_map/bksv,bs->bkv/dot_general | solution.py:72
  138.9 7.0 %scatter_custom_fusion.1 = f32[4096,128]{1,0:T(8,128)} fusion(s32[2048]{0:T(1024)S(1)} %bitcast.42, f32[2048,128]{1,0:T(8,128)S(1)} %bitcast.35, f32[]{:T(128)} %constant.23.clone.1), kind=kCustom, calls=%fused_computation.40 | custom fusion | bytes 2097156 | tf_op jit(solution)/shard_map/scatter | solution.py:75
  145.8 4.6 %all-to-all-start.2 = ((f32[128,32,128]{2,1,0:T(8,128)}), f32[128,32,128]{2,1,0:T(8,128)S(1)}, u32[]{:S(2)}, u32[]{:S(2)}) async-start(f32[128,32,128]{2,1,0:T(8,128)} %bitcast.18), calls=%async_computation.2 | async-start | bytes 4194304 | tf_op jit(solution)/shard_map/all_to_all | solution.py:76
  151.6 1.4 collective-permute-start.4
  153.0 4.0 %collective-permute-start.5 = (f32[1,64,512]{2,1,0:T(8,128)S(1)}, f32[1,64,512]{2,1,0:T(8,128)S(1)}, u32[]{:S(2)}, u32[]{:S(2)}) collective-permute-start(f32[1,64,512]{2,1,0:T(8,128)S(1)} %get-tuple-element.12), channel_id=1, source_target_pairs={{0,8},{8,16},{16,24},{24,32},{32,40},{40,48},{48,56},{56,64},{64,7... | collective-permute-start | bytes 393224 | tf_op jit(solution)/shard_map/ppermute | solution.py:18
  157.0 20.2 %collective-permute-done.4 = f32[1,64,512]{2,1,0:T(8,128)S(1)} collective-permute-done((f32[1,64,512]{2,1,0:T(8,128)S(1)}, f32[1,64,512]{2,1,0:T(8,128)S(1)}, u32[]{:S(2)}, u32[]{:S(2)}) %collective-permute-start.4) | collective-permute-done | bytes 131104 | tf_op jit(solution)/shard_map/ppermute | solution.py:19
  177.3 1.3 pad_maximum_fusion.14
  178.6 2.8 %collective-permute-start.6 = (f32[34,1,512]{2,0,1:T(8,128)S(1)}, f32[34,1,512]{2,0,1:T(8,128)S(1)}, u32[]{:S(2)}, u32[]{:S(2)}) collective-permute-start(f32[34,1,512]{2,0,1:T(8,128)S(1)} %copy.43), channel_id=1, source_target_pairs={{1,0},{2,1},{3,2},{4,3},{5,4},{6,5},{7,6},{9,8},{10,9},{11,10},{12... | collective-permute-start | bytes 208904 | tf_op jit(solution)/shard_map/ppermute | solution.py:19
  181.4 3.3 %collective-permute-start.7 = (f32[34,1,512]{2,0,1:T(8,128)S(1)}, f32[34,1,512]{2,0,1:T(8,128)S(1)}, u32[]{:S(2)}, u32[]{:S(2)}) collective-permute-start(f32[34,1,512]{2,0,1:T(8,128)S(1)} %copy.45), channel_id=1, source_target_pairs={{0,1},{1,2},{2,3},{3,4},{4,5},{5,6},{6,7},{8,9},{9,10},{10,11},{11... | collective-permute-start | bytes 208904 | tf_op jit(solution)/shard_map/ppermute | solution.py:18
  184.7 4.8 %fusion.34 = (f32[32,64,511]{2,1,0:T(8,128)}, f32[32,64,511]{2,1,0:T(8,128)}) fusion(f32[32,64,512]{2,1,0:T(8,128)S(1)} %copy-done), kind=kLoop, calls=%fused_computation.89 | loop fusion | bytes 16744448 | tf_op jit(solution)/shard_map/slice | solution.py:29
  189.7 24.6 %scatter_custom_fusion.2 = f32[8192,128]{1,0:T(8,128)} fusion(s32[4096]{0:T(1024)S(1)} %bitcast.44, f32[4096,128]{1,0:T(8,128)S(1)} %bitcast.36, f32[]{:T(128)} %constant.23.clone.1), kind=kCustom, calls=%fused_computation.34 | custom fusion | flops 524288 | bytes 4194308 | tf_op jit(solution)/shard_map/scatter-add | solution.py:90
  214.3 4.9 %reshape.227 = f32[32,64,512]{2,1,0:T(8,128)} reshape(f32[8192,128]{1,0:T(8,128)} %scatter_custom_fusion.2) | data formatting | bytes 8388608 | tf_op jit(solution)/shard_map/reshape | solution.py:92
  219.2 17.9 %fusion.7 = f32[32,64,512]{2,1,0:T(8,128)} fusion(f32[32,64,512]{2,1,0:T(8,128)} %param.6, f32[34,1,512]{2,1,0:T(1,128)S(1)} %copy.46, f32[1,64,512]{2,1,0:T(8,128)S(1)} %collective-permute-done.4, f32[32,64,512]{2,1,0:T(8,128)} %get-tuple-element.9, f32[1,64,512]{2,1,0:T(8,128)S(1)} %collective-permute-done.5, f32[34,1,512]{2,1,0:T(1,128)S(1)} %copy.44, ...), kind=kLoop, calls=%fused_computation.13 | loop fusion | flops 20971520 | bytes 25550848 | tf_op jit(solution)/shard_map/sub | solution.py:93
  (60 shorter events, 7.8 us)
Async XLA Ops:
  1.6 39.7 %collective-permute-start.1 = (f32[1,64,512]{2,1,0:T(8,128)S(1)}, f32[1,64,512]{2,1,0:T(8,128)S(1)}, u32[]{:S(2)}, u32[]{:S(2)}) collective-permute-start(f32[1,64,512]{2,1,0:T(8,128)S(1)} %get-tuple-element.17), channel_id=1, source_target_pairs={{0,8},{8,16},{16,24},{24,32},{32,40},{40,48},{48,56},{56,64},{64,7... | collective-permute-start | bytes 393224 | tf_op jit(solution)/shard_map/ppermute | solution.py:18
  5.7 38.5 %collective-permute-start = (f32[1,64,512]{2,1,0:T(8,128)S(1)}, f32[1,64,512]{2,1,0:T(8,128)S(1)}, u32[]{:S(2)}, u32[]{:S(2)}) collective-permute-start(f32[1,64,512]{2,1,0:T(8,128)S(1)} %get-tuple-element.16), channel_id=1, source_target_pairs={{8,0},{16,8},{24,16},{32,24},{40,32},{48,40},{56,48},{64,56},{72,6... | collective-permute-start | bytes 393224 | tf_op jit(solution)/shard_map/ppermute | solution.py:19
  18.4 21.4 %all-to-all-start = ((s32[128,1,32]{2,1,0:T(1,128)}), s32[128,1,32]{2,1,0:T(1,128)S(1)}, u32[]{:S(2)}, u32[]{:S(2)}) async-start(s32[128,1,32]{2,1,0:T(1,128)} %bitcast.5), calls=%async_computation | async-start | bytes 131072 | tf_op jit(solution)/shard_map/all_to_all | solution.py:50
  44.2 2.1 copy-start.1
  46.4 5.8 %collective-permute-start.2 = (f32[34,1,512]{2,0,1:T(8,128)S(1)}, f32[34,1,512]{2,0,1:T(8,128)S(1)}, u32[]{:S(2)}, u32[]{:S(2)}) collective-permute-start(f32[34,1,512]{2,0,1:T(8,128)S(1)} %copy.39), channel_id=1, source_target_pairs={{1,0},{2,1},{3,2},{4,3},{5,4},{6,5},{7,6},{9,8},{10,9},{11,10},{12... | collective-permute-start | bytes 208904 | tf_op jit(solution)/shard_map/ppermute | solution.py:19
  49.5 3.9 %collective-permute-start.3 = (f32[34,1,512]{2,0,1:T(8,128)S(1)}, f32[34,1,512]{2,0,1:T(8,128)S(1)}, u32[]{:S(2)}, u32[]{:S(2)}) collective-permute-start(f32[34,1,512]{2,0,1:T(8,128)S(1)} %copy.41), channel_id=1, source_target_pairs={{0,1},{1,2},{2,3},{3,4},{4,5},{5,6},{6,7},{8,9},{9,10},{10,11},{11... | collective-permute-start | bytes 208904 | tf_op jit(solution)/shard_map/ppermute | solution.py:18
  87.4 28.7 %all-to-all-start.1 = ((bf16[128,32,128]{2,1,0:T(8,128)(2,1)}), bf16[128,32,128]{2,1,0:T(8,128)(2,1)S(1)}, u32[]{:S(2)}, u32[]{:S(2)}) async-start(bf16[128,32,128]{2,1,0:T(8,128)(2,1)} %broadcast_select_fusion), calls=%async_computation.1 | async-start | bytes 2097152 | tf_op jit(solution)/shard_map/all_to_all | solution.py:59
  122.3 8.3 %copy-start.3 = (f32[64,32]{0,1:T(8,128)S(1)}, f32[64,32]{0,1:T(8,128)}, u32[]{:S(2)}) copy-start(f32[64,32]{0,1:T(8,128)} %param.9) | copy-start | bytes 24580
  122.3 8.3 %copy-start.4 = (f32[64,32]{0,1:T(8,128)S(1)}, f32[64,32]{0,1:T(8,128)}, u32[]{:S(2)}) copy-start(f32[64,32]{0,1:T(8,128)} %param.8) | copy-start | bytes 24580
  122.4 8.3 %copy-start.5 = (s32[64]{0:T(128)S(1)}, s32[64]{0:T(128)}, u32[]{:S(2)}) copy-start(s32[64]{0:T(128)} %param.10) | copy-start | bytes 772
  130.7 8.2 %copy-start.2 = (f32[64,1,32,1]{0,2,1,3:T(8,128)}, f32[64,1,32,1]{0,2,1,3:T(8,128)S(1)}, u32[]{:S(2)}) copy-start(f32[64,1,32,1]{0,2,1,3:T(8,128)S(1)} %copy.48) | copy-start | bytes 24580
  145.8 43.8 %all-to-all-start.2 = ((f32[128,32,128]{2,1,0:T(8,128)}), f32[128,32,128]{2,1,0:T(8,128)S(1)}, u32[]{:S(2)}, u32[]{:S(2)}) async-start(f32[128,32,128]{2,1,0:T(8,128)} %bitcast.18), calls=%async_computation.2 | async-start | bytes 4194304 | tf_op jit(solution)/shard_map/all_to_all | solution.py:76
  150.5 34.2 %copy-start = (f32[32,64,512]{2,1,0:T(8,128)S(1)}, f32[32,64,512]{2,1,0:T(8,128)}, u32[]{:S(2)}) copy-start(f32[32,64,512]{2,1,0:T(8,128)} %get-tuple-element.9) | copy-start | bytes 12582916
  151.6 25.7 %collective-permute-start.4 = (f32[1,64,512]{2,1,0:T(8,128)S(1)}, f32[1,64,512]{2,1,0:T(8,128)S(1)}, u32[]{:S(2)}, u32[]{:S(2)}) collective-permute-start(f32[1,64,512]{2,1,0:T(8,128)S(1)} %get-tuple-element.13), channel_id=1, source_target_pairs={{8,0},{16,8},{24,16},{32,24},{40,32},{48,40},{56,48},{64,56},{72,6... | collective-permute-start | bytes 393224 | tf_op jit(solution)/shard_map/ppermute | solution.py:19
  153.0 24.2 %collective-permute-start.5 = (f32[1,64,512]{2,1,0:T(8,128)S(1)}, f32[1,64,512]{2,1,0:T(8,128)S(1)}, u32[]{:S(2)}, u32[]{:S(2)}) collective-permute-start(f32[1,64,512]{2,1,0:T(8,128)S(1)} %get-tuple-element.12), channel_id=1, source_target_pairs={{0,8},{8,16},{16,24},{24,32},{32,40},{40,48},{48,56},{56,64},{64,7... | collective-permute-start | bytes 393224 | tf_op jit(solution)/shard_map/ppermute | solution.py:18
  178.6 10.9 %collective-permute-start.6 = (f32[34,1,512]{2,0,1:T(8,128)S(1)}, f32[34,1,512]{2,0,1:T(8,128)S(1)}, u32[]{:S(2)}, u32[]{:S(2)}) collective-permute-start(f32[34,1,512]{2,0,1:T(8,128)S(1)} %copy.43), channel_id=1, source_target_pairs={{1,0},{2,1},{3,2},{4,3},{5,4},{6,5},{7,6},{9,8},{10,9},{11,10},{12... | collective-permute-start | bytes 208904 | tf_op jit(solution)/shard_map/ppermute | solution.py:19
  181.4 8.1 %collective-permute-start.7 = (f32[34,1,512]{2,0,1:T(8,128)S(1)}, f32[34,1,512]{2,0,1:T(8,128)S(1)}, u32[]{:S(2)}, u32[]{:S(2)}) collective-permute-start(f32[34,1,512]{2,0,1:T(8,128)S(1)} %copy.45), channel_id=1, source_target_pairs={{0,1},{1,2},{2,3},{3,4},{4,5},{5,6},{6,7},{8,9},{9,10},{10,11},{11... | collective-permute-start | bytes 208904 | tf_op jit(solution)/shard_map/ppermute | solution.py:18
where the time goes:
time: 239 us; the launch traced here: 237 us
  local copies, waits for them, and re-layouts  64.8 us (27%)
  other arithmetic  64.4 us (27%)
  starting transfers between devices  48.4 us (20%)
  waiting for transfers between devices  42 us (18%)
  matrix products  16.3 us (7%)
    scatter-add x1, other arithmetic, on_device(): jnp.zeros((local_blocks, width), jnp.float32).at[slot_target]  24.6 us
    ppermute x4, waiting for transfers between devices, extended(): after = lax.ppermute(first, axis, down)  20.3 us
    all_to_all x1, waiting for transfers between devices, on_device(): lax.all_to_all(served.reshape(devices, capacity, width), ('gx', 'gy'), sp...  19.3 us
    sub x1, other arithmetic, on_device(): log_density - step_rate * (data_grad + prior_weight * prior_grad)  17.9 us
    convert_element_type x1, other arithmetic, on_device(): table = dens_field.astype(jnp.bfloat16).reshape(local_blocks, width)  16.6 us
    ppermute x4, starting transfers between devices, extended(): before = lax.ppermute(last, axis, up)  13.7 us
    slice x2, local copies, waits for them, and re-layouts, apply_op(): beside = beside + jnp.concatenate([center[:, :, 1:], blank_plane], 2)  12.9 us
    gather x1, local copies, waits for them, and re-layouts, on_device(): table[jnp.maximum(incoming, 0)]  12.1 us
  transfers between devices with their start and end apart: 11, of which 4 were waited for; matrix products, arithmetic and copies ran while one was open for 13% of the time, Pallas kernels for 0%

commit v1 on v0

v1 whole, which is shorter than its diff:
```python
import functools

import jax
import jax.numpy as jnp
from jax import lax
from jax.experimental import pallas as pl
from jax.experimental.pallas import tpu as pltpu
from jax.sharding import PartitionSpec as P

MESH = pl.DeviceIdType.MESH
DMA = pltpu.SemaphoreType.DMA
shift_kappa = 0.5
prior_weight = 0.05
step_rate = 2.0
f32, bf16, i32 = jnp.float32, jnp.bfloat16, jnp.int32

NDEV, CAP, WIDTH = 128, 32, 128
BLOCKS, SLOTS, STARS = 64, 32, 32
REQ = BLOCKS * SLOTS
CX, CY, NZ = 32, 64, 512
LOCAL_BITS = 13


def vmem(shape, dtype):
    return pltpu.VMEM(shape, dtype)


def whole(space):
    return pl.BlockSpec(memory_space=space)


def bucket_kernel(ids_ref, out_ref, inv_ref, pos_ref, at_ref, bt_ref):
    ids = ids_ref[...]
    target = ids >> LOCAL_BITS
    within = ids & ((1 << LOCAL_BITS) - 1)
    order = lax.broadcasted_iota(i32, (1, REQ), 1)
    at = lax.broadcasted_iota(i32, (NDEV, REQ), 0) == target
    at_ref[...] = jnp.where(at, 1.0, 0.0).astype(bf16)
    step = 256
    before = (lax.broadcasted_iota(i32, (step, step), 0) < lax.broadcasted_iota(i32, (step, step), 1))
    before = jnp.where(before, 1.0, 0.0).astype(bf16)
    running = jnp.zeros((NDEV, 1), f32)
    slot = lax.broadcasted_iota(i32, (CAP, step), 0)
    for k in range(REQ // step):
        cut = slice(k * step, (k + 1) * step)
        part = at_ref[:, cut]
        prefix = jnp.dot(part, before, preferred_element_type=f32) + running
        wide = part.astype(f32)
        rank = jnp.sum(wide * prefix, axis=0, keepdims=True).astype(i32)
        running = running + jnp.sum(wide, axis=1, keepdims=True)
        hit = slot == rank
        pos_ref[:, cut] = target[:, cut] * CAP + rank
        for n, value in enumerate((within[:, cut] >> 7, within[:, cut] & 127, order[:, cut] >> 7, order[:, cut] & 127, None)):
            value = 1.0 if value is None else value.astype(f32)
            bt_ref[n * CAP:(n + 1) * CAP, cut] = jnp.where(hit, value, 0.0).astype(bf16)
    table = lax.dot_general(at_ref[...], bt_ref[...], (((1,), (1,)), ((), ())), preferred_element_type=f32)
    parts = [table[:, n * CAP:(n + 1) * CAP] for n in range(5)]
    present = parts[4] > 0.5
    out_ref[...] = jnp.where(present, parts[0] * 128.0 + parts[1], -1.0).astype(i32)[:, None, :]
    inv_ref[...] = jnp.where(present, parts[2] * 128.0 + parts[3], float(REQ)).astype(i32)


def bucket(block_ids):
    return pl.pallas_call(
        bucket_kernel,
        out_shape=(
            jax.ShapeDtypeStruct((NDEV, 1, CAP), i32),
            jax.ShapeDtypeStruct((NDEV, CAP), i32),
            jax.ShapeDtypeStruct((1, REQ), i32),
        ),
        in_specs=[whole(pltpu.VMEM)],
        out_specs=[whole(pltpu.VMEM)] * 3,
        scratch_shapes=[vmem((NDEV, REQ), bf16), vmem((5 * CAP, REQ), bf16)],
        name="bucket",
    )(block_ids.reshape(1, REQ))


def position_tables():
    gx, gy = lax.axis_index("gx"), lax.axis_index("gy")
    around = lambda v, n: [lax.rem(v + d, n) for d in range(n)]
    return gx, gy, around(gx // 4, 4), around(lax.rem(gx, 4), 4), around(gy // 2, 4), around(lax.rem(gy, 2), 2)


def signal_all(tables):
    gx, gy, xs, ys, zs, cs = tables
    barrier = pltpu.get_barrier_semaphore()
    for j in range(1, NDEV):
        pl.semaphore_signal(
            barrier, inc=1, device_id=(xs[j // 32] * 4 + ys[j // 8 % 4], zs[j // 2 % 4] * 2 + cs[j % 2]), device_id_type=MESH
        )


def wait_all():
    pl.semaphore_wait(pltpu.get_barrier_semaphore(), NDEV - 1)


def peer(gx, gy, j):
    o = lax.rem(j * 37, NDEV)
    x = lax.rem(gx // 4 + o // 32, 4)
    y = lax.rem(gx + lax.rem(o // 8, 4), 4)
    z = lax.rem(gy // 2 + lax.rem(o // 2, 4), 4)
    c = lax.rem(gy + o, 2)
    return x * 4 + y, z * 2 + c


def remote(src, dst, send, recv, to):
    return pltpu.make_async_remote_copy(
        src_ref=src, dst_ref=dst, send_sem=send, recv_sem=recv, device_id=to, device_id_type=MESH
    )


def drain(ref, sem):
    pltpu.make_async_copy(ref, ref, sem).wait()


def fetch_kernel(out_ids, dens_hbm, ret_ref, in_ids, exp_ref, xlo, xhi, ylo, yhi,
                 dens, served, ids_smem, s_id, r_id, s_row, r_row, local, s_halo, r_halo):
    tables = position_tables()
    gx, gy, xs, ys, zs, cs = tables
    me = gx * 8 + gy
    loads = [pltpu.make_async_copy(dens_hbm.at[:, :, pl.ds(q * WIDTH, WIDTH)], dens.at[q], local.at[q]) for q in range(4)]
    for load in loads:
        load.start()
    signal_all(tables)
    wait_all()
    own = pltpu.make_async_copy(out_ids.at[me], in_ids.at[me], local.at[4])
    own.start()
    for j in range(1, NDEV):
        tx, ty = xs[j // 32] * 4 + ys[j // 8 % 4], zs[j // 2 % 4] * 2 + cs[j % 2]
        remote(out_ids.at[tx * 8 + ty], in_ids.at[me], s_id, r_id, (tx, ty)).start()
    gxm, gxp = lax.rem(gx + 15, 16), lax.rem(gx + 1, 16)
    gym, gyp = lax.rem(gy + 7, 8), lax.rem(gy + 1, 8)
    halos = [
        (dens_hbm.at[pl.ds(CX - 2, 2)], xlo, (gxp, gy)),
        (dens_hbm.at[pl.ds(0, 2)], xhi, (gxm, gy)),
        (dens_hbm.at[:, pl.ds(CY - 8, 8)], ylo.at[pl.ds(1, CX)], (gx, gyp)),
        (dens_hbm.at[:, pl.ds(0, 8)], yhi.at[pl.ds(1, CX)], (gx, gym)),
        (dens_hbm.at[CX - 1, pl.ds(CY - 8, 8)], ylo.at[0], (gxp, gyp)),
        (dens_hbm.at[0, pl.ds(CY - 8, 8)], ylo.at[CX + 1], (gxm, gyp)),
        (dens_hbm.at[CX - 1, pl.ds(0, 8)], yhi.at[0], (gxp, gym)),
        (dens_hbm.at[0, pl.ds(0, 8)], yhi.at[CX + 1], (gxm, gym)),
    ]
    halos = [remote(src, dst, s_halo.at[n], r_halo.at[n], to) for n, (src, dst, to) in enumerate(halos)]
    own.wait()
    drain(in_ids.at[pl.ds(0, NDEV - 1)], r_id)
    to_smem = pltpu.make_async_copy(in_ids, ids_smem, local.at[4])
    to_smem.start()
    for copy in halos:
        copy.start()
    to_smem.wait()
    for load in loads:
        load.wait()

    def serve(at):
        for c in range(CAP):
            n = jnp.maximum(ids_smem[at, 0, c], 0)
            exp_ref[at, c, :] = dens[n & 3, n >> 8, (n >> 2) & 63, :]
        rows = jnp.exp(exp_ref[at])
        exp_ref[at] = rows
        served[at] = rows.astype(bf16)

    def send(j, _):
        tx, ty = peer(gx, gy, j)
        at = tx * 8 + ty
        serve(at)
        remote(served.at[at], ret_ref.at[me], s_row, r_row, (tx, ty)).start()
        return 0

    lax.fori_loop(1, NDEV, send, 0)
    serve(me)
    keep = pltpu.make_async_copy(served.at[me], ret_ref.at[me], local.at[0])
    keep.start()
    keep.wait()
    drain(out_ids.at[pl.ds(0, NDEV - 1)], s_id)
    for copy in halos:
        copy.wait()
    drain(served.at[pl.ds(0, NDEV - 1)], s_row)
    drain(ret_ref.at[pl.ds(0, NDEV - 1)], r_row)


def fetch(out_ids, dens):
    return pl.pallas_call(
        fetch_kernel,
        out_shape=(
            jax.ShapeDtypeStruct((NDEV, CAP, WIDTH), bf16),
            jax.ShapeDtypeStruct((NDEV, 1, CAP), i32),
            jax.ShapeDtypeStruct((NDEV, CAP, WIDTH), f32),
            jax.ShapeDtypeStruct((2, CY, NZ), f32),
            jax.ShapeDtypeStruct((2, CY, NZ), f32),
            jax.ShapeDtypeStruct((CX + 2, 8, NZ), f32),
            jax.ShapeDtypeStruct((CX + 2, 8, NZ), f32),
        ),
        in_specs=[whole(pltpu.VMEM), whole(pl.ANY)],
        out_specs=[whole(pltpu.VMEM)] * 7,
        scratch_shapes=[
            vmem((4, CX, CY, WIDTH), f32), vmem((NDEV, CAP, WIDTH), bf16), pltpu.SMEM((NDEV, 1, CAP), i32),
            DMA, DMA, DMA, DMA, DMA((5,)), DMA((8,)), DMA((8,)),
        ],
        name="fetch",
        compiler_params=pltpu.CompilerParams(collective_id=0, has_side_effects=True, vmem_limit_bytes=40 << 20),
    )(out_ids, dens)


CHUNK = 8


def stars_kernel(pos, counts, ret, weights, observed, inverse_var, ext_ref, sens_ref, rows, stage, obs4, inv4):
    step = pl.program_id(0)

    @pl.when(step == 0)
    def _():
        rows[...] = ret[...].astype(f32).reshape(NDEV * CAP, WIDTH)
        obs4[...] = jnp.concatenate([observed[...]] * 4, axis=1)
        inv4[...] = jnp.concatenate([inverse_var[...]] * 4, axis=1)
        sens_ref[pl.ds(REQ, 8), :] = jnp.zeros((8, WIDTH), f32)

    group = lax.broadcasted_iota(i32, (SLOTS, SLOTS * STARS), 1) >> 5
    mine = group == lax.broadcasted_iota(i32, (SLOTS, SLOTS * STARS), 0)
    star = lax.broadcasted_iota(i32, (1, WIDTH), 1) & (STARS - 1)
    for u in range(CHUNK):
        b = step * CHUNK + u
        for k in range(SLOTS):
            stage[u, k, :] = rows[pos[0, b * SLOTS + k], :]
        values = stage[u].astype(bf16)
        w = weights[u].reshape(SLOTS * STARS, WIDTH)
        every = lax.dot_general(values, w, (((1,), (1,)), ((), ())), preferred_element_type=f32)
        every = jnp.sum(jnp.where(mine, every, 0.0), axis=0, keepdims=True)
        tiles = [every[:, n * WIDTH:(n + 1) * WIDTH] for n in range(SLOTS * STARS // WIDTH)]
        while len(tiles) > 1:
            tiles = [tiles[n] + tiles[n + 1] for n in range(0, len(tiles), 2)]
        ext = tiles[0]
        ext = ext + pltpu.roll(ext, 64, 1)
        ext = ext + pltpu.roll(ext, 32, 1)
        ext_ref[pl.ds(b, 1), :] = ext[:, :STARS]
        weighted = jnp.where(star < counts[b], inv4[pl.ds(b, 1), :] * (ext - obs4[pl.ds(b, 1), :]), 0.0)
        spread = jnp.concatenate([weighted] * 8, axis=1)
        left = jnp.where(mine, spread, 0.0).astype(bf16)
        sens_ref[pl.ds(b * SLOTS, SLOTS), :] = jnp.dot(left, w, preferred_element_type=f32)


def stars_step(pos, counts, ret, weights, observed, inverse_var):
    fixed = lambda i: (0, 0)
    return pl.pallas_call(
        stars_kernel,
        grid=(BLOCKS // CHUNK,),
        out_shape=(jax.ShapeDtypeStruct((BLOCKS, STARS), f32), jax.ShapeDtypeStruct((REQ + 8, WIDTH), f32)),
        in_specs=[
            whole(pltpu.SMEM), whole(pltpu.SMEM), whole(pltpu.VMEM),
            pl.BlockSpec((CHUNK, SLOTS, STARS, WIDTH), lambda i: (i, 0, 0, 0)),
            whole(pltpu.VMEM), whole(pltpu.VMEM),
        ],
        out_specs=[pl.BlockSpec((BLOCKS, STARS), fixed), pl.BlockSpec((REQ + 8, WIDTH), fixed)],
        scratch_shapes=[vmem((NDEV * CAP, WIDTH), f32), vmem((CHUNK, SLOTS, WIDTH), f32), vmem((BLOCKS, WIDTH), f32), vmem((BLOCKS, WIDTH), f32)],
        name="stars",
        compiler_params=pltpu.CompilerParams(dimension_semantics=("arbitrary",), vmem_limit_bytes=32 << 20),
    )(pos, counts, ret, weights, observed, inverse_var)


def return_kernel(inv, sens, arr_ref, stage, parcel, s_row, r_row, local):
    tables = position_tables()
    gx, gy = tables[:2]
    me = gx * 8 + gy
    signal_all(tables)
    wait_all()

    def pack(at):
        for c in range(CAP):
            stage[c, :] = sens[inv[at, c], :]
        parcel[at] = stage[...].astype(bf16)

    def send(j, _):
        tx, ty = peer(gx, gy, j)
        at = tx * 8 + ty
        pack(at)
        remote(parcel.at[at], arr_ref.at[me], s_row, r_row, (tx, ty)).start()
        return 0

    lax.fori_loop(1, NDEV, send, 0)
    pack(me)
    keep = pltpu.make_async_copy(parcel.at[me], arr_ref.at[me], local)
    keep.start()
    keep.wait()
    drain(parcel.at[pl.ds(0, NDEV - 1)], s_row)
    drain(arr_ref.at[pl.ds(0, NDEV - 1)], r_row)


def give_back(inv, sens):
    return pl.pallas_call(
        return_kernel,
        out_shape=jax.ShapeDtypeStruct((NDEV, CAP, WIDTH), bf16),
        in_specs=[whole(pltpu.SMEM), whole(pltpu.VMEM)],
        out_specs=whole(pltpu.VMEM),
        scratch_shapes=[vmem((CAP, WIDTH), f32), vmem((NDEV, CAP, WIDTH), bf16), DMA, DMA, DMA],
        name="give_back",
        compiler_params=pltpu.CompilerParams(collective_id=1, has_side_effects=True, vmem_limit_bytes=16 << 20),
    )(inv, sens)


def update_kernel(ids, dens, xlo, xhi, ylo, yhi, rows_exp, arrived, out_hbm, smooth, add, new, sem):
    gx, gy = lax.axis_index("gx"), lax.axis_index("gy")
    TALL = CY + 16
    lane = lax.broadcasted_iota(i32, (TALL, NZ), 1)
    row = lax.broadcasted_iota(i32, (TALL, NZ), 0)
    inside = ((row >= 8) | (gy > 0)) & ((row < CY + 8) | (gy < 7))
    low, high = lane == 0, lane == NZ - 1

    def apply(center, before, after):
        side = before + after
        side = side + pltpu.roll(center, 1, 0) + pltpu.roll(center, TALL - 1, 0)
        side = side + jnp.where(low, 0.0, pltpu.roll(center, 1, 1))
        side = side + jnp.where(high, 0.0, pltpu.roll(center, NZ - 1, 1))
        return (shift_kappa + 6.0) * center - side

    def plane(body, lo, hi):
        return jnp.where(inside, jnp.concatenate([lo, body, hi], axis=0), 0.0)

    blank = jnp.zeros((8, NZ), f32)
    at_low, at_high = gx == 0, gx == 15

    def outer(body, lo, hi, gone):
        return jnp.where(gone, 0.0, plane(body, lo, hi))

    e_m2 = outer(xlo[0], blank, blank, at_low)
    e_m1 = outer(xlo[1], ylo[0], yhi[0], at_low)
    e_p0 = outer(xhi[0], ylo[CX + 1], yhi[CX + 1], at_high)
    e_p1 = outer(xhi[1], blank, blank, at_high)

    def inner(x):
        return plane(dens[x], ylo[x + 1], yhi[x + 1])

    smooth[0] = jnp.where(inside & (gx > 0), apply(e_m1, e_m2, inner(0)), 0.0)
    smooth[1] = jnp.where(inside, apply(inner(0), e_m1, inner(1)), 0.0)

    def middle(x, _):
        smooth[x + 1] = jnp.where(inside, apply(inner(x), inner(x - 1), inner(x + 1)), 0.0)
        return 0

    lax.fori_loop(1, CX - 1, middle, 0)
    smooth[CX] = jnp.where(inside, apply(inner(CX - 1), inner(CX - 2), e_p0), 0.0)
    smooth[CX + 1] = jnp.where(inside & (gx < 15), apply(e_p0, inner(CX - 1), e_p1), 0.0)

    def last(x, _):
        prior = apply(smooth[x + 1], smooth[x], smooth[x + 2])
        fresh = dens[x] - (step_rate * prior_weight) * prior[8:8 + CY]
        for q in range(4):
            new[q, x] = fresh[:, q * WIDTH:(q + 1) * WIDTH]
        return 0

    lax.fori_loop(0, CX, last, 0)

    def scale(t, _):
        add[t] = step_rate * rows_exp[t] * arrived[t].astype(f32)
        return 0

    lax.fori_loop(0, NDEV, scale, 0)

    def source(t, _):
        for g in range(CAP // 8):
            @pl.when(ids[t, 0, g * 8] >= 0)
            def _():
                for c in range(g * 8, g * 8 + 8):
                    n = jnp.maximum(ids[t, 0, c], 0)
                    at = (n & 3, n >> 8, (n >> 2) & 63)
                    new[at] = new[at] - add[t, c, :]
        return 0

    lax.fori_loop(0, NDEV, source, 0)
    stores = [pltpu.make_async_copy(new.at[q], out_hbm.at[:, :, pl.ds(q * WIDTH, WIDTH)], sem.at[q]) for q in range(4)]
    for store in stores:
        store.start()
    for store in stores:
        store.wait()


def update(ids, dens, xlo, xhi, ylo, yhi, rows_exp, arrived):
    return pl.pallas_call(
        update_kernel,
        out_shape=jax.ShapeDtypeStruct((CX, CY, NZ), f32),
        in_specs=[whole(pltpu.SMEM)] + [whole(pltpu.VMEM)] * 7,
        out_specs=whole(pl.ANY),
        scratch_shapes=[
            vmem((CX + 2, CY + 16, NZ), f32), vmem((NDEV, CAP, WIDTH), f32), vmem((4, CX, CY, WIDTH), f32), DMA((4,)),
        ],
        name="update",
        compiler_params=pltpu.CompilerParams(vmem_limit_bytes=40 << 20),
    )(ids, dens, xlo, xhi, ylo, yhi, rows_exp, arrived)


def on_device(log_density, weights, observed, inverse_var, star_counts, block_ids):
    out_ids, inv, pos = bucket(block_ids)
    ret, in_ids, rows_exp, xlo, xhi, ylo, yhi = fetch(out_ids, log_density)
    extinction, sens = stars_step(pos, star_counts, ret, weights, observed, inverse_var)
    arrived = give_back(inv, sens)
    new = update(in_ids, log_density, xlo, xhi, ylo, yhi, rows_exp, arrived)
    return (new, extinction)


def solution(mesh):
    placed = (
        P("gx", "gy", None),
        P(("gx", "gy"), None, None, None),
        P(("gx", "gy"), None),
        P(("gx", "gy"), None),
        P(("gx", "gy")),
        P(("gx", "gy"), None),
    )
    return jax.shard_map(
        on_device,
        mesh=mesh,
        in_specs=placed,
        out_specs=(P("gx", "gy", None), P(("gx", "gy"), None)),
        check_vma=False,
    )
```

time: 239 us -> 137 us (0.57)
  Pallas kernels: 0 us -> 123 us
  other arithmetic: 64.4 us -> 0 us
  local copies, waits for them, and re-layouts: 64.8 us -> 12.6 us
  starting transfers between devices: 48.4 us -> 0 us
  waiting for transfers between devices: 42 us -> 0 us
  matrix products: 16.3 us -> 0 us
    pallas_call x0 -> x5, Pallas kernels: none -> 123 us  [the longest x1 42.4 us: fetch(): pl.pallas_call(fetch_kernel, out_shape=(jax.ShapeDtypeStruct((NDEV, CAP,...]
    all_to_all x3 -> x0, starting transfers between devices: 26.1 us -> none  [the longest x1 12 us: on_device(): lax.all_to_all(outgoing.reshape(devices, capacity), ('gx', 'gy'), split_a...]
    scatter-add x1 -> x0, other arithmetic: 24.6 us -> none  [on_device(): jnp.zeros((local_blocks, width), jnp.float32).at[slot_target]]
    ppermute x8 -> x0, starting transfers between devices: 22.3 us -> none  [the longest x4 13.7 us: extended(): before = lax.ppermute(last, axis, up)]
    ppermute x8 -> x0, waiting for transfers between devices: 21.5 us -> none  [the longest x4 20.3 us: extended(): after = lax.ppermute(first, axis, down)]
    all_to_all x3 -> x0, waiting for transfers between devices: 20.5 us -> none  [the longest x1 19.3 us: on_device(): lax.all_to_all(served.reshape(devices, capacity, width), ('gx', 'gy'), sp...]
    gather x2 -> x0, local copies, waits for them, and re-layouts: 18.3 us -> none  [the longest x1 12.1 us: on_device(): table[jnp.maximum(incoming, 0)]]
    sub x2 -> x0, other arithmetic: 17.9 us -> none  [the longest x1 17.9 us: on_device(): log_density - step_rate * (data_grad + prior_weight * prior_grad)]
  transfers between devices with their start and end apart: 11 -> 0, of which waited for: 4 -> 0; matrix products, arithmetic and copies ran while one was open for 13% -> 0% of each run, Pallas kernels for 0% -> 0%
where the time goes in v1:
time: 137 us; the launch traced here: 136 us
  Pallas kernels  123 us (90%)
  local copies, waits for them, and re-layouts  12.6 us (9%)
    pallas_call x1, Pallas kernels, fetch(): pl.pallas_call(fetch_kernel, out_shape=(jax.ShapeDtypeStruct((NDEV, CAP,...  42.4 us
    pallas_call x1, Pallas kernels, update(): pl.pallas_call(update_kernel, out_shape=jax.ShapeDtypeStruct((CX, CY, NZ)...  29.3 us
    pallas_call x1, Pallas kernels, stars_step(): pl.pallas_call(stars_kernel, grid=(BLOCKS // CHUNK,), out_shape=(jax.Shap...  26.5 us
    pallas_call x1, Pallas kernels, give_back(): pl.pallas_call(return_kernel, out_shape=jax.ShapeDtypeStruct((NDEV, CAP,...  22.7 us
    unnamed x18, local copies, waits for them, and re-layouts  11.9 us

profile of v1, /device:TPU:1, one launch (start us, length us, event | category | flops | bytes accessed | tf_op | source)
XLA Modules:
  0.0 136.4 jit_solution(2873293653749926637)
XLA Ops:
  0.6 0.0 copy-start.6
  0.6 0.8 copy.13.observed
  1.4 0.8 copy.14.inverse_var
  2.2 0.8 copy.12
  3.0 0.7 reshape.7.ids_ref
  3.7 2.2 %bucket.1 = (s32[128,1,32]{2,1,0:T(1,128)}, s32[128,32]{1,0:T(8,128)}, s32[1,2048]{1,0:T(1,128)}) custom-call(s32[1,2048]{1,0:T(1,128)} %reshape.7.ids_ref), custom_call_target="tpu_custom_call" | custom-call | tf_op jit(solution)/shard_map/bucket/pallas_call | solution.py:64
  5.9 0.0 copy-start
  5.9 2.2 %copy-done = f32[32,64,512]{2,1,0:T(8,128)S(1)} copy-done((f32[32,64,512]{2,1,0:T(8,128)S(1)}, f32[32,64,512]{2,1,0:T(8,128)}, u32[]{:S(2)}) %copy-start) | copy-done | bytes 4194328
  8.1 0.0 copy-start.3
  8.1 0.8 copy-done.3
  8.9 0.0 copy-start.5
  8.9 42.4 %fetch.1 = (bf16[128,32,128]{2,1,0:T(8,128)(2,1)S(1)}, s32[128,1,32]{2,1,0:T(1,128)S(1)}, f32[128,32,128]{2,1,0:T(8,128)S(1)}, f32[2,64,512]{2,1,0:T(8,128)S(1)}...) custom-call(s32[128,1,32]{2,1,0:T(1,128)S(1)} %copy-done.3, ...), custom_call_target="tpu_custom_call" | custom-call | tf_op jit(solution)/shard_map/fetch/pallas_call | solution.py:182
  51.4 0.0 copy-done.6
  51.4 0.0 copy-done.5
  51.4 0.0 copy-start.2
  51.4 5.8 %copy-done.2 = bf16[64,32,32,128]{3,2,1,0:T(8,128)(2,1)S(1)} copy-done((bf16[64,32,32,128]{3,2,1,0:T(8,128)(2,1)S(1)}, bf16[64,32,32,128]{3,2,1,0:T(8,128)(2,1)}, u32[]{:S(2)}) %copy-start.2) | copy-done | bytes 16777240
  57.1 0.0 copy-start.4
  57.2 0.0 copy-start.1
  57.2 26.5 %stars.1 = (f32[64,32]{1,0:T(8,128)S(1)}, f32[2056,128]{1,0:T(8,128)S(1)}) custom-call(s32[1,2048]{1,0:T(1,128)S(1)} %copy-done.5, s32[64]{0:T(128)S(1)} %copy-done.6, bf16[128,32,128]{2,1,0:T(8,128)(2,1)S(1)} %get-tuple-element.23.ret, bf16[64,32,32,128]{3,2,1,0:T(8,128)(2,1)S(1)} %copy-done.2, f32[64,32]{1,0:T(8,128)S(1)} %copy.13.observed, ...), custom_call_target="tpu_custom_call" | custom-call | tf_op jit(solution)/shard_map/stars/pallas_call | solution.py:243
  83.6 0.0 copy-done.4
  83.6 22.7 %give_back.1.arrived = bf16[128,32,128]{2,1,0:T(8,128)(2,1)S(1)} custom-call(s32[128,32]{1,0:T(8,128)S(1)} %copy-done.4, f32[2056,128]{1,0:T(8,128)S(1)} %get-tuple-element.24.sens), custom_call_target="tpu_custom_call" | custom-call | tf_op jit(solution)/shard_map/give_back/pallas_call | solution.py:288
  106.3 0.0 copy-done.1
  106.3 29.3 %update.1 = f32[32,64,512]{2,1,0:T(8,128)} custom-call(s32[128,1,32]{2,1,0:T(1,128)S(1)} %get-tuple-element.15.ids, f32[32,64,512]{2,1,0:T(8,128)S(1)} %copy-done.1, f32[2,64,512]{2,1,0:T(8,128)S(1)} %get-tuple-element.16.xlo, f32[2,64,512]{2,1,0:T(8,128)S(1)} %get-tuple-element.17.xhi, f32[34,8,512]{2,1,0:T(8,128)S(1)} %get-tuple-element.18.ylo, ...), custom_call_target="tpu_custom_call" | custom-call | tf_op jit(solution)/shard_map/update/pallas_call | solution.py:376
  135.7 0.7 copy.15
Async XLA Ops:
  0.6 50.7 %copy-start.6 = (s32[64]{0:T(128)S(1)}, s32[64]{0:T(128)}, u32[]{:S(2)}) copy-start(s32[64]{0:T(128)} %counts.1) | copy-start | bytes 772
  5.9 2.2 %copy-start = (f32[32,64,512]{2,1,0:T(8,128)S(1)}, f32[32,64,512]{2,1,0:T(8,128)}, u32[]{:S(2)}) copy-start(f32[32,64,512]{2,1,0:T(8,128)} %dens.1) | copy-start | bytes 12582916
  8.1 0.8 copy-start.3
  8.9 42.5 %copy-start.5 = (s32[1,2048]{1,0:T(1,128)S(1)}, s32[1,2048]{1,0:T(1,128)}, u32[]{:S(2)}) copy-start(s32[1,2048]{1,0:T(1,128)} %get-tuple-element.22.pos) | copy-start | bytes 24580
  51.4 5.8 %copy-start.2 = (bf16[64,32,32,128]{3,2,1,0:T(8,128)(2,1)S(1)}, bf16[64,32,32,128]{3,2,1,0:T(8,128)(2,1)}, u32[]{:S(2)}) copy-start(bf16[64,32,32,128]{3,2,1,0:T(8,128)(2,1)} %weights.1) | copy-start | bytes 50331652
  57.1 26.5 %copy-start.4 = (s32[128,32]{1,0:T(8,128)S(1)}, s32[128,32]{1,0:T(8,128)}, u32[]{:S(2)}) copy-start(s32[128,32]{1,0:T(8,128)} %get-tuple-element.21.inv) | copy-start | bytes 49156
  57.2 49.2 %copy-start.1 = (f32[32,64,512]{2,1,0:T(8,128)S(1)}, f32[32,64,512]{2,1,0:T(8,128)}, u32[]{:S(2)}) copy-start(f32[32,64,512]{2,1,0:T(8,128)} %dens.1) | copy-start | bytes 12582916

commit v2 on v0

v2 whole, which is shorter than its diff:
```python
import jax
import jax.numpy as jnp
from jax import lax
from jax.experimental import pallas as pl
from jax.experimental.pallas import tpu as pltpu
from jax.sharding import PartitionSpec as P

MESH = pl.DeviceIdType.MESH
DMA = pltpu.SemaphoreType.DMA
shift_kappa = 0.5
prior_weight = 0.05
step_rate = 2.0
f32, bf16, i32 = jnp.float32, jnp.bfloat16, jnp.int32

GX, GY = 16, 8
NDEV, CAP, WIDTH = 128, 32, 128
BLOCKS, SLOTS, STARS = 64, 32, 32
REQ = BLOCKS * SLOTS
CX, CY, ZB = 32, 64, 4
ROWS = CX * CY * ZB
LOCAL_BITS = 13
UNROLL = 4
center_weight = shift_kappa + 6.0


def whole(space):
    return pl.BlockSpec(memory_space=space)


def remote(src, dst, send, recv, to):
    return pltpu.make_async_remote_copy(
        src_ref=src, dst_ref=dst, send_sem=send, recv_sem=recv, device_id=to, device_id_type=MESH
    )


def drain(ref, sem):
    pltpu.make_async_copy(ref, ref, sem).wait()


def peer(gx, gy, j):
    o = lax.rem(j * 37, NDEV)
    x = lax.rem(gx // 4 + o // 32, 4)
    y = lax.rem(gx + lax.rem(o // 8, 4), 4)
    z = lax.rem(gy // 2 + lax.rem(o // 2, 4), 4)
    c = lax.rem(gy + o, 2)
    return x * 4 + y, z * 2 + c


def bucket_kernel(blocks, out_ids, inv_ref, pos_ref, at_ref, bt_ref):
    ids = jnp.concatenate([blocks[k:k + 1, :] for k in range(SLOTS)], axis=1)
    target = ids >> LOCAL_BITS
    within = ids & (ROWS - 1)
    within = (within & (ZB - 1)) * (CX * CY) + (within >> 2)
    order = lax.broadcasted_iota(i32, (1, REQ), 1)
    order = (order & (BLOCKS - 1)) * SLOTS + (order >> 6)
    at_ref[...] = jnp.where(lax.broadcasted_iota(i32, (NDEV, REQ), 0) == target, 1.0, 0.0).astype(bf16)
    step = 256
    before = lax.broadcasted_iota(i32, (step, step), 0) < lax.broadcasted_iota(i32, (step, step), 1)
    before = jnp.where(before, 1.0, 0.0).astype(bf16)
    running = jnp.zeros((NDEV, 1), f32)
    slot = lax.broadcasted_iota(i32, (CAP, step), 0)
    for k in range(REQ // step):
        cut = slice(k * step, (k + 1) * step)
        part = at_ref[:, cut]
        prefix = jnp.dot(part, before, preferred_element_type=f32) + running
        wide = part.astype(f32)
        rank = jnp.sum(wide * prefix, axis=0, keepdims=True).astype(i32)
        running = running + jnp.sum(wide, axis=1, keepdims=True)
        hit = slot == rank
        pos_ref[:, cut] = target[:, cut] * CAP + rank
        for n, value in enumerate((within[:, cut] >> 7, within[:, cut] & 127, order[:, cut] >> 7, order[:, cut] & 127, None)):
            value = 1.0 if value is None else value.astype(f32)
            bt_ref[n * CAP:(n + 1) * CAP, cut] = jnp.where(hit, value, 0.0).astype(bf16)
    table = lax.dot_general(at_ref[...], bt_ref[...], (((1,), (1,)), ((), ())), preferred_element_type=f32)
    parts = [table[:, n * CAP:(n + 1) * CAP] for n in range(5)]
    present = parts[4] > 0.5
    row = jnp.where(present, parts[0] * 128.0 + parts[1], float(ROWS)).astype(i32)
    out_ids[...] = row.reshape(GX, GY, 1, CAP)
    inv_ref[...] = jnp.where(present, parts[2] * 128.0 + parts[3], float(REQ)).astype(i32)


def bucket(blocks):
    shape, v = jax.ShapeDtypeStruct, pltpu.VMEM
    return pl.pallas_call(
        bucket_kernel,
        out_shape=(shape((GX, GY, 1, CAP), i32), shape((NDEV, CAP), i32), shape((1, REQ), i32)),
        in_specs=[whole(v)],
        out_specs=[whole(v)] * 3,
        scratch_shapes=[v((NDEV, REQ), bf16), v((5 * CAP, REQ), bf16)],
        name="bucket",
    )(blocks)


def shifted_sum(field, x, row):
    lane = lax.broadcasted_iota(i32, (8, WIDTH), 1)
    first, final = lane == 0, lane == WIDTH - 1
    at = lambda q, dx, dr: field[q, x + dx, pl.ds(row + dr, 8), :]
    centers = [at(q, 0, 0) for q in range(ZB)]
    up = [pltpu.roll(c, 1, 1) for c in centers]
    down = [pltpu.roll(c, WIDTH - 1, 1) for c in centers]
    sides = []
    for q in range(ZB):
        below = jnp.where(first, up[q - 1] if q > 0 else 0.0, up[q])
        above = jnp.where(final, down[q + 1] if q < ZB - 1 else 0.0, down[q])
        sides.append((at(q, -1, 0) + at(q, 1, 0)) + (at(q, 0, -1) + at(q, 0, 1)) + (below + above))
    return centers, sides


def step_kernel(out_ids, inv_s, pos_s, dens_hbm, weights_hbm, counts, observed, inverse_var,
                ext_out, ids_out, exp_hbm, same_out, base_hbm, arr_hbm,
                dens, mid_ids, in_ids, ids_s,
                rows_exp, served, ret, rows, w_ref, obs4, inv4, ext4, wgt4, sens, stage, parcel,
                xlo, xhi, ylo, yhi, field, smooth, base,
                entered, s_id, r_id, s_row, r_row, local, s_halo, r_halo):
    gx, gy = lax.axis_index("gx"), lax.axis_index("gy")
    me = gx * GY + gy
    gxm, gxp = lax.rem(gx + GX - 1, GX), lax.rem(gx + 1, GX)
    gym, gyp = lax.rem(gy + GY - 1, GY), lax.rem(gy + 1, GY)
    column = [lax.rem(gx + d, GX) for d in (1, 15, 4, 12, 3, 13, 5, 11, 7, 9, 2, 14, 6, 10, 8)]
    line = [lax.rem(gy + d, GY) for d in (1, 7, 2, 6, 3, 5, 4)]
    greeted = [(t, gy) for t in column] + [(gx, t) for t in line] + [(a, b) for a in (gxm, gxp) for b in (gym, gyp)]
    barrier = pltpu.get_barrier_semaphore()
    for to in greeted:
        pl.semaphore_signal(barrier, inc=1, device_id=to, device_id_type=MESH)

    loads = []
    for q in range(ZB):
        part = dens_hbm.at[:, :, pl.ds(q * WIDTH, WIDTH)]
        loads.append(pltpu.make_async_copy(part, field.at[q, pl.ds(2, CX), pl.ds(8, CY)], local.at[q]))
    w_load = pltpu.make_async_copy(weights_hbm, w_ref, local.at[4])
    for load in loads:
        load.start()
    w_load.start()

    pl.semaphore_wait(barrier, len(greeted))
    for t in line:
        pl.semaphore_signal(entered, inc=1, device_id=(gx, t), device_id_type=MESH)
    own = pltpu.make_async_copy(out_ids.at[gx], mid_ids.at[gx], local.at[7])
    own.start()
    for t in column:
        remote(out_ids.at[t], mid_ids.at[gx], s_id.at[0], r_id.at[0], (t, gy)).start()

    for load in loads:
        load.wait()
    halos = [
        (field.at[:, pl.ds(CX, 2), pl.ds(8, CY)], xlo, (gxp, gy)),
        (field.at[:, pl.ds(2, 2), pl.ds(8, CY)], xhi, (gxm, gy)),
        (field.at[:, pl.ds(2, CX), pl.ds(CY, 8)], ylo.at[:, pl.ds(1, CX)], (gx, gyp)),
        (field.at[:, pl.ds(2, CX), pl.ds(8, 8)], yhi.at[:, pl.ds(1, CX)], (gx, gym)),
        (field.at[:, CX + 1, pl.ds(CY, 8)], ylo.at[:, 0], (gxp, gyp)),
        (field.at[:, 2, pl.ds(CY, 8)], ylo.at[:, CX + 1], (gxm, gyp)),
        (field.at[:, CX + 1, pl.ds(8, 8)], yhi.at[:, 0], (gxp, gym)),
        (field.at[:, 2, pl.ds(8, 8)], yhi.at[:, CX + 1], (gxm, gym)),
    ]
    halos = [remote(src, dst, s_halo.at[n], r_halo.at[n], to) for n, (src, dst, to) in enumerate(halos)]

    def gather_source(x, _):
        for q in range(ZB):
            dens[pl.ds(pl.multiple_of(q * CX * CY + x * CY, CY), CY), :] = field[q, x + 2, pl.ds(8, CY), :]
        return 0

    lax.fori_loop(0, CX, gather_source, 0)
    dens[pl.ds(ROWS, 8), :] = jnp.zeros((8, WIDTH), f32)
    own.wait()
    drain(mid_ids.at[pl.ds(0, GX - 1)], r_id.at[0])
    pl.semaphore_wait(entered, len(line))
    own = pltpu.make_async_copy(mid_ids.at[:, gy], in_ids.at[:, gy], local.at[7])
    own.start()
    for t in line:
        remote(mid_ids.at[:, t], in_ids.at[:, gy], s_id.at[1], r_id.at[1], (gx, t)).start()
    for copy in halos:
        copy.start()

    for ref, four in ((observed, obs4), (inverse_var, inv4)):
        wide = jnp.concatenate([ref[...], ref[...]], axis=1)
        four[...] = jnp.concatenate([wide] * 4, axis=0).T
    sens[pl.ds(REQ, 8), :] = jnp.zeros((8, WIDTH), f32)
    own.wait()
    drain(in_ids.at[:, pl.ds(0, GY - 1)], r_id.at[1])
    ids_copy = pltpu.make_async_copy(in_ids, ids_s, local.at[7])
    ids_copy.start()
    ids_copy.wait()
    slot_a, slot_b = lax.broadcasted_iota(i32, (CAP, CAP), 0), lax.broadcasted_iota(i32, (CAP, CAP), 1)
    eye, together = slot_a == slot_b, (slot_a >> 3) == (slot_b >> 3)

    def serve(tx, ty, at):
        for c in range(CAP):
            rows_exp[at, c, :] = dens[ids_s[tx, ty, 0, c], :]
        values = jnp.exp(rows_exp[at])
        rows_exp[at] = values
        served[at] = values.astype(bf16)
        across = jnp.broadcast_to(in_ids[tx, ty].astype(f32), (CAP, CAP))
        down = jnp.sum(jnp.where(eye, across, 0.0), axis=1, keepdims=True)
        same_out[at] = jnp.where((down == across) & together, 1.0, 0.0).astype(bf16)

    def send_rows(j, _):
        tx, ty = peer(gx, gy, j)
        at = tx * GY + ty
        serve(tx, ty, at)
        remote(served.at[at], ret.at[me], s_row.at[0], r_row.at[0], (tx, ty)).start()
        return 0

    lax.fori_loop(1, NDEV, send_rows, 0)
    serve(gx, gy, me)
    keep = pltpu.make_async_copy(served.at[me], ret.at[me], local.at[0])
    keep.start()
    ids_out[...] = in_ids[...]
    exp_store = pltpu.make_async_copy(rows_exp, exp_hbm, local.at[1])
    exp_store.start()

    for copy in halos:
        copy.wait()
    low_x, high_x, low_y, high_y = gx > 0, gx < GX - 1, gy > 0, gy < GY - 1
    blank = jnp.zeros((8, WIDTH), f32)
    for q in range(ZB):
        for n in range(2):
            field[q, n, pl.ds(8, CY), :] = jnp.where(low_x, xlo[q, n], 0.0)
            field[q, CX + 2 + n, pl.ds(8, CY), :] = jnp.where(high_x, xhi[q, n], 0.0)

        def edge(x, _):
            field[q, x + 1, pl.ds(0, 8), :] = jnp.where(low_y, ylo[q, x], 0.0)
            field[q, x + 1, pl.ds(8 + CY, 8), :] = jnp.where(high_y, yhi[q, x], 0.0)
            return 0

        lax.fori_loop(1, CX + 1, edge, 0)
        for x, inside in ((0, low_x), (CX + 1, high_x)):
            field[q, x + 1, pl.ds(0, 8), :] = jnp.where(low_y & inside, ylo[q, x], 0.0)
            field[q, x + 1, pl.ds(8 + CY, 8), :] = jnp.where(high_y & inside, yhi[q, x], 0.0)
    sub = lax.broadcasted_iota(i32, (8, WIDTH), 0)
    top_keep = (sub > 0) | low_y
    bottom_keep = (sub != 1) | high_y

    def smooth_plane(x, inside=None):
        for n in range(9):
            centers, sides = shifted_sum(field, x + 1, 7 + 8 * n)
            for q in range(ZB):
                value = center_weight * centers[q] - sides[q]
                if n == 0:
                    value = jnp.where(top_keep, value, 0.0)
                if n == 8:
                    value = jnp.where(bottom_keep, value, 0.0)
                if inside is not None:
                    value = jnp.where(inside, value, 0.0)
                smooth[q, x, pl.ds(8 * n, 8), :] = value

    def base_plane(x):
        for n in range(8):
            centers, sides = shifted_sum(smooth, x + 1, 8 * n + 1)
            for q in range(ZB):
                prior = center_weight * centers[q] - sides[q]
                now = field[q, x + 2, pl.ds(8 + 8 * n, 8), :]
                base[q, x, pl.ds(8 * n, 8), :] = now - (step_rate * prior_weight) * prior

    smooth_plane(0, low_x)
    smooth_plane(1)
    smooth_plane(2)
    w_load.wait()
    keep.wait()
    drain(ret.at[pl.ds(0, NDEV - 1)], r_row.at[0])

    def widen(n, _):
        for u in range(UNROLL):
            rows[pl.ds(pl.multiple_of((n * UNROLL + u) * CAP, CAP), CAP), :] = ret[n * UNROLL + u].astype(f32)
        return 0

    lax.fori_loop(0, NDEV // UNROLL, widen, 0)
    group = lax.broadcasted_iota(i32, (SLOTS, SLOTS * STARS), 1) >> 5
    mine = group == lax.broadcasted_iota(i32, (SLOTS, SLOTS * STARS), 0)
    lane = lax.broadcasted_iota(i32, (STARS, WIDTH), 1)
    diagonal = (lane & (STARS - 1)) == lax.broadcasted_iota(i32, (STARS, WIDTH), 0)
    star = lax.broadcasted_iota(i32, (1, WIDTH), 1) & (STARS - 1)

    def extinct(i):
        for u in range(UNROLL):
            b = i * UNROLL + u
            totals = [jnp.zeros((STARS, WIDTH), f32) for _ in range(2)]
            for k in range(SLOTS):
                line_k = rows[pl.ds(pos_s[0, k * BLOCKS + b], 1), :]
                totals[k % 2] = totals[k % 2] + w_ref[b, k].astype(f32) * line_k
            total = jnp.sum(totals[0] + totals[1], axis=1, keepdims=True)
            ext = jnp.sum(jnp.where(diagonal, total, 0.0), axis=0, keepdims=True)
            ext4[pl.ds(b, 1), :] = ext
            residual = inv4[pl.ds(b, 1), :] * (ext - obs4[pl.ds(b, 1), :])
            wgt4[pl.ds(b, 1), :] = jnp.where(star < counts[b], residual, 0.0)

    def sensitive(i):
        for u in range(UNROLL):
            b = i * UNROLL + u
            spread = jnp.concatenate([wgt4[pl.ds(b, 1), :]] * (SLOTS * STARS // WIDTH), axis=1)
            left = jnp.where(mine, spread, 0.0).astype(bf16)
            sens[pl.ds(pl.multiple_of(b * SLOTS, SLOTS), SLOTS), :] = jnp.dot(
                left, w_ref[b].reshape(SLOTS * STARS, WIDTH), preferred_element_type=f32
            )

    extinct(0)

    def both(i, _):
        sensitive(i - 1)
        extinct(i)
        return 0

    lax.fori_loop(1, BLOCKS // UNROLL, both, 0)
    sensitive(BLOCKS // UNROLL - 1)

    def pack(at):
        for c in range(CAP):
            stage[at, c, :] = sens[inv_s[at, c], :]
        parcel[at] = stage[at].astype(bf16)

    def give_back(it, _):
        for u in range(UNROLL):
            j = it * UNROLL + u + 1
            tx, ty = peer(gx, gy, j)
            at = tx * GY + ty
            pack(at)
            remote(parcel.at[at], arr_hbm.at[me], s_row.at[1], r_row.at[1], (tx, ty)).start()
        smooth_plane(it + 3, (it < CX - 2) | high_x)
        base_plane(it)
        return 0

    def last_trip():
        for u in range(UNROLL):
            j = NDEV - UNROLL + u + 1
            tx, ty = peer(gx, gy, j)
            at = tx * GY + ty
            pack(at)
            if u < UNROLL - 1:
                remote(parcel.at[at], arr_hbm.at[me], s_row.at[1], r_row.at[1], (tx, ty)).start()
        base_plane(CX - 1)

    lax.fori_loop(0, NDEV // UNROLL - 1, give_back, 0)
    last_trip()
    keep = pltpu.make_async_copy(parcel.at[me], arr_hbm.at[me], local.at[0])
    keep.start()
    base_store = pltpu.make_async_copy(base, base_hbm, local.at[2])
    base_store.start()
    ext_out[...] = jnp.concatenate([ext4[...], ext4[...]], axis=0).T[:STARS, :BLOCKS]
    keep.wait()
    exp_store.wait()
    base_store.wait()
    drain(out_ids.at[pl.ds(0, GX - 1)], s_id.at[0])
    drain(mid_ids.at[:, pl.ds(0, GY - 1)], s_id.at[1])
    drain(served.at[pl.ds(0, NDEV - 1)], s_row.at[0])
    drain(parcel.at[pl.ds(0, NDEV - 1)], s_row.at[1])
    drain(arr_hbm.at[pl.ds(0, NDEV - 1)], r_row.at[1])


def step(ids, inv, pos, dens, weights, counts, observed, inverse_var):
    shape = jax.ShapeDtypeStruct
    v = pltpu.VMEM
    return pl.pallas_call(
        step_kernel,
        out_shape=(
            shape((STARS, BLOCKS), f32),
            shape((GX, GY, 1, CAP), i32),
            shape((NDEV, CAP, WIDTH), f32),
            shape((NDEV, CAP, CAP), bf16),
            shape((ZB, CX, CY, WIDTH), f32),
            shape((NDEV, CAP, WIDTH), bf16),
        ),
        in_specs=[
            whole(v), whole(pltpu.SMEM), whole(pltpu.SMEM),
            whole(pltpu.HBM), whole(pltpu.HBM), whole(pltpu.SMEM), whole(v), whole(v),
        ],
        out_specs=[whole(v), whole(v), whole(pltpu.HBM), whole(v), whole(pltpu.HBM), whole(pltpu.HBM)],
        scratch_shapes=[
            v((ROWS + 8, WIDTH), f32),
            v((GX, GY, 1, CAP), i32), v((GX, GY, 1, CAP), i32), pltpu.SMEM((GX, GY, 1, CAP), i32),
            v((NDEV, CAP, WIDTH), f32), v((NDEV, CAP, WIDTH), bf16), v((NDEV, CAP, WIDTH), bf16),
            v((NDEV * CAP, WIDTH), f32), v((BLOCKS, SLOTS, STARS, WIDTH), bf16),
            v((WIDTH, WIDTH), f32), v((WIDTH, WIDTH), f32), v((BLOCKS, WIDTH), f32), v((BLOCKS, WIDTH), f32),
            v((REQ + 8, WIDTH), f32), v((NDEV, CAP, WIDTH), f32), v((NDEV, CAP, WIDTH), bf16),
            v((ZB, 2, CY, WIDTH), f32), v((ZB, 2, CY, WIDTH), f32),
            v((ZB, CX + 2, 8, WIDTH), f32), v((ZB, CX + 2, 8, WIDTH), f32),
            v((ZB, CX + 4, CY + 16, WIDTH), f32), v((ZB, CX + 2, CY + 8, WIDTH), f32), v((ZB, CX, CY, WIDTH), f32),
            pltpu.SemaphoreType.REGULAR, DMA((2,)), DMA((2,)), DMA((2,)), DMA((2,)), DMA((8,)), DMA((8,)), DMA((8,)),
        ],
        name="step",
        compiler_params=pltpu.CompilerParams(collective_id=0, has_side_effects=True, vmem_limit_bytes=60 << 20),
    )(ids, inv, pos, dens, weights, counts, observed, inverse_var)


def update_kernel(ids, ext_in, exp_hbm, same, base_hbm, arr_hbm, ext_out, out_hbm, new, rows_exp, arrived, add, sem):
    load_exp = pltpu.make_async_copy(exp_hbm, rows_exp, sem.at[0])
    load_arr = pltpu.make_async_copy(arr_hbm, arrived, sem.at[1])
    load_exp.start()
    load_arr.start()
    bases = []
    for q in range(ZB):
        bases.append(pltpu.make_async_copy(base_hbm.at[q], new.at[pl.ds(q * CX * CY, CX * CY)], sem.at[2 + q]))
        bases[q].start()
    ext_out[...] = ext_in[...]
    new[pl.ds(ROWS, 8), :] = jnp.zeros((8, WIDTH), f32)
    load_exp.wait()
    load_arr.wait()

    def scale(n, _):
        for u in range(UNROLL):
            t = n * UNROLL + u
            add[t] = step_rate * rows_exp[t] * jnp.dot(same[t], arrived[t], preferred_element_type=f32)
        return 0

    lax.fori_loop(0, NDEV // UNROLL, scale, 0)
    for load in bases:
        load.wait()

    def source(t, _):
        tx, ty = t // GY, lax.rem(t, GY)
        for first in range(0, CAP, 8):
            at = [ids[tx, ty, 0, first + c] for c in range(8)]
            values = [new[pl.ds(n, 1), :] - add[t, pl.ds(first + c, 1), :] for c, n in enumerate(at)]
            for n, value in zip(at, values):
                new[pl.ds(n, 1), :] = value
        return 0

    lax.fori_loop(0, NDEV, source, 0)
    stores = []
    for q in range(ZB):
        rows_of = new.at[pl.ds(q * CX * CY, CX * CY)]
        stores.append(pltpu.make_async_copy(
            rows_of.reshape(CX, CY, WIDTH), out_hbm.at[:, :, pl.ds(q * WIDTH, WIDTH)], sem.at[2 + q]
        ))
        stores[q].start()
    for store in stores:
        store.wait()


def update(ids, ext, rows_exp, same, base, arrived):
    v = pltpu.VMEM
    return pl.pallas_call(
        update_kernel,
        out_shape=(jax.ShapeDtypeStruct((STARS, BLOCKS), f32), jax.ShapeDtypeStruct((CX, CY, ZB * WIDTH), f32)),
        in_specs=[whole(pltpu.SMEM), whole(v), whole(pltpu.HBM), whole(v), whole(pltpu.HBM), whole(pltpu.HBM)],
        out_specs=[whole(v), whole(pltpu.HBM)],
        scratch_shapes=[
            v((ROWS + 8, WIDTH), f32), v((NDEV, CAP, WIDTH), f32), v((NDEV, CAP, WIDTH), bf16), v((NDEV, CAP, WIDTH), f32),
            DMA((6,)),
        ],
        name="update",
        compiler_params=pltpu.CompilerParams(vmem_limit_bytes=24 << 20),
    )(ids, ext, rows_exp, same, base.reshape(ZB, CX * CY, WIDTH), arrived)


def on_device(log_density, weights, observed, inverse_var, star_counts, block_ids):
    ids, inv, pos = bucket(block_ids.T)
    ext, ids, rows_exp, same, base, arrived = step(
        ids, inv, pos, log_density, weights, star_counts, observed.T, inverse_var.T
    )
    ext, new = update(ids, ext, rows_exp, same, base, arrived)
    return (new, ext.T)


def solution(mesh):
    placed = (
        P("gx", "gy", None),
        P(("gx", "gy"), None, None, None),
        P(("gx", "gy"), None),
        P(("gx", "gy"), None),
        P(("gx", "gy")),
        P(("gx", "gy"), None),
    )
    return jax.shard_map(
        on_device,
        mesh=mesh,
        in_specs=placed,
        out_specs=(P("gx", "gy", None), P(("gx", "gy"), None)),
        check_vma=False,
    )
```

time: 239 us -> 93.7 us (0.39)
  Pallas kernels: 0 us -> 84.7 us
  other arithmetic: 64.4 us -> 0 us
  local copies, waits for them, and re-layouts: 64.8 us -> 7.78 us
  starting transfers between devices: 48.4 us -> 0 us
  waiting for transfers between devices: 42 us -> 0 us
  matrix products: 16.3 us -> 0 us
    pallas_call x0 -> x3, Pallas kernels: none -> 84.7 us  [the longest x1 66.9 us: step(): pl.pallas_call(step_kernel, out_shape=(shape((STARS, BLOCKS), f32), shape...]
    all_to_all x3 -> x0, starting transfers between devices: 26.1 us -> none  [the longest x1 12 us: on_device(): lax.all_to_all(outgoing.reshape(devices, capacity), ('gx', 'gy'), split_a...]
    scatter-add x1 -> x0, other arithmetic: 24.6 us -> none  [on_device(): jnp.zeros((local_blocks, width), jnp.float32).at[slot_target]]
    ppermute x8 -> x0, starting transfers between devices: 22.3 us -> none  [the longest x4 13.7 us: extended(): before = lax.ppermute(last, axis, up)]
    ppermute x8 -> x0, waiting for transfers between devices: 21.5 us -> none  [the longest x4 20.3 us: extended(): after = lax.ppermute(first, axis, down)]
    all_to_all x3 -> x0, waiting for transfers between devices: 20.5 us -> none  [the longest x1 19.3 us: on_device(): lax.all_to_all(served.reshape(devices, capacity, width), ('gx', 'gy'), sp...]
    gather x2 -> x0, local copies, waits for them, and re-layouts: 18.3 us -> none  [the longest x1 12.1 us: on_device(): table[jnp.maximum(incoming, 0)]]
    sub x2 -> x0, other arithmetic: 17.9 us -> none  [the longest x1 17.9 us: on_device(): log_density - step_rate * (data_grad + prior_weight * prior_grad)]
  transfers between devices with their start and end apart: 11 -> 0, of which waited for: 4 -> 0; matrix products, arithmetic and copies ran while one was open for 13% -> 0% of each run, Pallas kernels for 0% -> 0%
where the time goes in v2:
time: 93.7 us; the launch traced here: 93.1 us
  Pallas kernels  84.7 us (90%)
  local copies, waits for them, and re-layouts  7.78 us (8%)
    pallas_call x1, Pallas kernels, step(): pl.pallas_call(step_kernel, out_shape=(shape((STARS, BLOCKS), f32), shape...  66.9 us
    pallas_call x1, Pallas kernels, update(): pl.pallas_call(update_kernel, out_shape=(jax.ShapeDtypeStruct((STARS, BLO...  15.6 us
    unnamed x12, local copies, waits for them, and re-layouts  7.78 us
    pallas_call x1, Pallas kernels, bucket(): pl.pallas_call(bucket_kernel, out_shape=(shape((GX, GY, 1, CAP), i32), sh...  2.23 us

profile of v2, /device:TPU:1, one launch (start us, length us, event | category | flops | bytes accessed | tf_op | source)
XLA Modules:
  0.0 93.1 jit_solution(8764734373171405643)
XLA Ops:
  0.6 2.2 %bucket.1 = (s32[16,8,1,32]{3,2,1,0:T(1,128)}, s32[128,32]{1,0:T(8,128)}, s32[1,2048]{1,0:T(1,128)}) custom-call(s32[32,64]{1,0:T(8,128)} %bitcast.6), custom_call_target="tpu_custom_call" | custom-call | tf_op jit(solution)/shard_map/bucket/pallas_call | solution.py:84
  2.9 66.9 %step.1 = (f32[32,64]{1,0:T(8,128)}, s32[16,8,1,32]{3,2,1,0:T(1,128)}, f32[128,32,128]{2,1,0:T(8,128)}, bf16[128,32,32]{2,1,0:T(8,128)(2,1)}, f32[4,32,64,128]{3,2,1,0:T(8,128)}, /*index=5*/bf16[128,32,128]{2,1,0:T(8,128)(2,1)}) custom-call(s32[16,8,1,32]{3,2,1,0:T(1,128)} %get-tuple-element.13.out_ids, s32[128,32]{1,0:T(8,128)} %get-tuple-element.14.inv_s, ...), custom_call_target="tpu_custom_call" | custom-call | tf_op jit(solution)/shard_map/step/pallas_call | solution.py:351
  69.8 0.0 copy-start
  69.8 2.2 %copy-done = f32[4,32,64,128]{3,2,1,0:T(8,128)S(1)} copy-done((f32[4,32,64,128]{3,2,1,0:T(8,128)S(1)}, f32[4,32,64,128]{3,2,1,0:T(8,128)}, u32[]{:S(2)}) %copy-start) | copy-done | bytes 4194328
  72.0 0.0 copy-start.1
  72.0 1.6 %copy-done.1 = f32[128,32,128]{2,1,0:T(8,128)S(1)} copy-done((f32[128,32,128]{2,1,0:T(8,128)S(1)}, f32[128,32,128]{2,1,0:T(8,128)}, u32[]{:S(2)}) %copy-start.1) | copy-done | bytes 2097176
  73.5 0.0 copy-start.2
  73.6 1.2 %copy-done.2 = bf16[128,32,32]{2,1,0:T(8,128)(2,1)S(1)} copy-done((bf16[128,32,32]{2,1,0:T(8,128)(2,1)S(1)}, bf16[128,32,32]{2,1,0:T(8,128)(2,1)}, u32[]{:S(2)}) %copy-start.2) | copy-done | bytes 262168
  74.8 0.0 copy-start.3
  74.8 1.2 %copy-done.3 = bf16[128,32,128]{2,1,0:T(8,128)(2,1)S(1)} copy-done((bf16[128,32,128]{2,1,0:T(8,128)(2,1)S(1)}, bf16[128,32,128]{2,1,0:T(8,128)(2,1)}, u32[]{:S(2)}) %copy-start.3) | copy-done | bytes 1048600
  76.0 0.0 copy-start.4
  76.0 0.8 copy-done.4
  76.8 0.0 copy-start.5
  76.8 0.7 copy-done.5
  77.6 15.6 %update.1 = (f32[32,64]{1,0:T(8,128)}, f32[32,64,512]{2,1,0:T(8,128)}) custom-call(s32[16,8,1,32]{3,2,1,0:T(1,128)S(1)} %copy-done.4, f32[32,64]{1,0:T(8,128)S(1)} %copy-done.5, f32[128,32,128]{2,1,0:T(8,128)S(1)} %copy-done.1, bf16[128,32,32]{2,1,0:T(8,128)(2,1)S(1)} %copy-done.2, f32[4,2048,128]{2,1,0:T(8,128)S(1)} %bitcast.5, ...), custom_call_target="tpu_custom_call" | custom-call | tf_op jit(solution)/shard_map/update/pallas_call | solution.py:430
Async XLA Ops:
  69.8 2.2 %copy-start = (f32[4,32,64,128]{3,2,1,0:T(8,128)S(1)}, f32[4,32,64,128]{3,2,1,0:T(8,128)}, u32[]{:S(2)}) copy-start(f32[4,32,64,128]{3,2,1,0:T(8,128)} %get-tuple-element.20) | copy-start | bytes 12582916
  72.0 1.6 %copy-start.1 = (f32[128,32,128]{2,1,0:T(8,128)S(1)}, f32[128,32,128]{2,1,0:T(8,128)}, u32[]{:S(2)}) copy-start(f32[128,32,128]{2,1,0:T(8,128)} %get-tuple-element.18.exp_hbm) | copy-start | bytes 6291460
  73.5 1.2 %copy-start.2 = (bf16[128,32,32]{2,1,0:T(8,128)(2,1)S(1)}, bf16[128,32,32]{2,1,0:T(8,128)(2,1)}, u32[]{:S(2)}) copy-start(bf16[128,32,32]{2,1,0:T(8,128)(2,1)} %get-tuple-element.19.same) | copy-start | bytes 786436
  74.8 1.2 %copy-start.3 = (bf16[128,32,128]{2,1,0:T(8,128)(2,1)S(1)}, bf16[128,32,128]{2,1,0:T(8,128)(2,1)}, u32[]{:S(2)}) copy-start(bf16[128,32,128]{2,1,0:T(8,128)(2,1)} %get-tuple-element.21.arr_hbm) | copy-start | bytes 3145732
  76.0 0.8 copy-start.4
  76.8 0.7 copy-start.5

commit v3 on v2

--- a/solution.py
+++ b/solution.py
@@ -107,7 +107,7 @@
 
 
 def step_kernel(out_ids, inv_s, pos_s, dens_hbm, weights_hbm, counts, observed, inverse_var,
-                ext_out, ids_out, exp_hbm, same_out, base_hbm, arr_hbm,
+                ext_out, ids_out, exp_hbm, base_hbm, arr_hbm,
                 dens, mid_ids, in_ids, ids_s,
                 rows_exp, served, ret, rows, w_ref, obs4, inv4, ext4, wgt4, sens, stage, parcel,
                 xlo, xhi, ylo, yhi, field, smooth, base,
@@ -180,18 +180,13 @@
     ids_copy = pltpu.make_async_copy(in_ids, ids_s, local.at[7])
     ids_copy.start()
     ids_copy.wait()
-    slot_a, slot_b = lax.broadcasted_iota(i32, (CAP, CAP), 0), lax.broadcasted_iota(i32, (CAP, CAP), 1)
-    eye, together = slot_a == slot_b, (slot_a >> 3) == (slot_b >> 3)
 
     def serve(tx, ty, at):
         for c in range(CAP):
             rows_exp[at, c, :] = dens[ids_s[tx, ty, 0, c], :]
         values = jnp.exp(rows_exp[at])
-        rows_exp[at] = values
+        rows_exp[at] = step_rate * values
         served[at] = values.astype(bf16)
-        across = jnp.broadcast_to(in_ids[tx, ty].astype(f32), (CAP, CAP))
-        down = jnp.sum(jnp.where(eye, across, 0.0), axis=1, keepdims=True)
-        same_out[at] = jnp.where((down == across) & together, 1.0, 0.0).astype(bf16)
 
     def send_rows(j, _):
         tx, ty = peer(gx, gy, j)
@@ -264,8 +259,8 @@
         return 0
 
     lax.fori_loop(0, NDEV // UNROLL, widen, 0)
-    group = lax.broadcasted_iota(i32, (SLOTS, SLOTS * STARS), 1) >> 5
-    mine = group == lax.broadcasted_iota(i32, (SLOTS, SLOTS * STARS), 0)
+    deep = 8 * STARS
+    mine = (lax.broadcasted_iota(i32, (8, deep), 1) >> 5) == lax.broadcasted_iota(i32, (8, deep), 0)
     lane = lax.broadcasted_iota(i32, (STARS, WIDTH), 1)
     diagonal = (lane & (STARS - 1)) == lax.broadcasted_iota(i32, (STARS, WIDTH), 0)
     star = lax.broadcasted_iota(i32, (1, WIDTH), 1) & (STARS - 1)
@@ -286,11 +281,12 @@
     def sensitive(i):
         for u in range(UNROLL):
             b = i * UNROLL + u
-            spread = jnp.concatenate([wgt4[pl.ds(b, 1), :]] * (SLOTS * STARS // WIDTH), axis=1)
-            left = jnp.where(mine, spread, 0.0).astype(bf16)
-            sens[pl.ds(pl.multiple_of(b * SLOTS, SLOTS), SLOTS), :] = jnp.dot(
-                left, w_ref[b].reshape(SLOTS * STARS, WIDTH), preferred_element_type=f32
-            )
+            line_b = wgt4[pl.ds(b, 1), :]
+            left = jnp.where(mine, jnp.concatenate([line_b, line_b], axis=1), 0.0).astype(bf16)
+            for n in range(SLOTS // 8):
+                sens[pl.ds(pl.multiple_of(b * SLOTS + n * 8, 8), 8), :] = jnp.dot(
+                    left, w_ref[b, pl.ds(n * 8, 8)].reshape(deep, WIDTH), preferred_element_type=f32
+                )
 
     extinct(0)
 
@@ -302,17 +298,23 @@
     lax.fori_loop(1, BLOCKS // UNROLL, both, 0)
     sensitive(BLOCKS // UNROLL - 1)
 
-    def pack(at):
+    slot_a, slot_b = lax.broadcasted_iota(i32, (CAP, CAP), 0), lax.broadcasted_iota(i32, (CAP, CAP), 1)
+    eye, together = slot_a == slot_b, (slot_a >> 3) == (slot_b >> 3)
+
+    def pack(tx, ty, at):
         for c in range(CAP):
             stage[at, c, :] = sens[inv_s[at, c], :]
-        parcel[at] = stage[at].astype(bf16)
+        across = jnp.broadcast_to(out_ids[tx, ty].astype(f32), (CAP, CAP))
+        down = jnp.sum(jnp.where(eye, across, 0.0), axis=1, keepdims=True)
+        same = jnp.where((down == across) & together, 1.0, 0.0).astype(bf16)
+        parcel[at] = jnp.dot(same, stage[at].astype(bf16), preferred_element_type=f32).astype(bf16)
 
     def give_back(it, _):
         for u in range(UNROLL):
             j = it * UNROLL + u + 1
             tx, ty = peer(gx, gy, j)
             at = tx * GY + ty
-            pack(at)
+            pack(tx, ty, at)
             remote(parcel.at[at], arr_hbm.at[me], s_row.at[1], r_row.at[1], (tx, ty)).start()
         smooth_plane(it + 3, (it < CX - 2) | high_x)
         base_plane(it)
@@ -323,7 +325,7 @@
             j = NDEV - UNROLL + u + 1
             tx, ty = peer(gx, gy, j)
             at = tx * GY + ty
-            pack(at)
+            pack(tx, ty, at)
             if u < UNROLL - 1:
                 remote(parcel.at[at], arr_hbm.at[me], s_row.at[1], r_row.at[1], (tx, ty)).start()
         base_plane(CX - 1)
@@ -354,7 +356,6 @@
             shape((STARS, BLOCKS), f32),
             shape((GX, GY, 1, CAP), i32),
             shape((NDEV, CAP, WIDTH), f32),
-            shape((NDEV, CAP, CAP), bf16),
             shape((ZB, CX, CY, WIDTH), f32),
             shape((NDEV, CAP, WIDTH), bf16),
         ),
@@ -362,7 +363,7 @@
             whole(v), whole(pltpu.SMEM), whole(pltpu.SMEM),
             whole(pltpu.HBM), whole(pltpu.HBM), whole(pltpu.SMEM), whole(v), whole(v),
         ],
-        out_specs=[whole(v), whole(v), whole(pltpu.HBM), whole(v), whole(pltpu.HBM), whole(pltpu.HBM)],
+        out_specs=[whole(v), whole(v), whole(pltpu.HBM), whole(pltpu.HBM), whole(pltpu.HBM)],
         scratch_shapes=[
             v((ROWS + 8, WIDTH), f32),
             v((GX, GY, 1, CAP), i32), v((GX, GY, 1, CAP), i32), pltpu.SMEM((GX, GY, 1, CAP), i32),
@@ -380,7 +381,7 @@
     )(ids, inv, pos, dens, weights, counts, observed, inverse_var)
 
 
-def update_kernel(ids, ext_in, exp_hbm, same, base_hbm, arr_hbm, ext_out, out_hbm, new, rows_exp, arrived, add, sem):
+def update_kernel(ids, ext_in, exp_hbm, base_hbm, arr_hbm, ext_out, out_hbm, new, rows_exp, arrived, add, sem):
     load_exp = pltpu.make_async_copy(exp_hbm, rows_exp, sem.at[0])
     load_arr = pltpu.make_async_copy(arr_hbm, arrived, sem.at[1])
     load_exp.start()
@@ -397,7 +398,7 @@
     def scale(n, _):
         for u in range(UNROLL):
             t = n * UNROLL + u
-            add[t] = step_rate * rows_exp[t] * jnp.dot(same[t], arrived[t], preferred_element_type=f32)
+            add[t] = rows_exp[t] * arrived[t].astype(f32)
         return 0
 
     lax.fori_loop(0, NDEV // UNROLL, scale, 0)
@@ -406,11 +407,24 @@
 
     def source(t, _):
         tx, ty = t // GY, lax.rem(t, GY)
-        for first in range(0, CAP, 8):
+
+        def eight(first):
             at = [ids[tx, ty, 0, first + c] for c in range(8)]
             values = [new[pl.ds(n, 1), :] - add[t, pl.ds(first + c, 1), :] for c, n in enumerate(at)]
             for n, value in zip(at, values):
                 new[pl.ds(n, 1), :] = value
+
+        eight(0)
+        eight(8)
+
+        @pl.when(ids[tx, ty, 0, 16] < ROWS)
+        def _():
+            eight(16)
+
+            @pl.when(ids[tx, ty, 0, 24] < ROWS)
+            def _():
+                eight(24)
+
         return 0
 
     lax.fori_loop(0, NDEV, source, 0)
@@ -425,28 +439,28 @@
         store.wait()
 
 
-def update(ids, ext, rows_exp, same, base, arrived):
+def update(ids, ext, rows_exp, base, arrived):
     v = pltpu.VMEM
     return pl.pallas_call(
         update_kernel,
         out_shape=(jax.ShapeDtypeStruct((STARS, BLOCKS), f32), jax.ShapeDtypeStruct((CX, CY, ZB * WIDTH), f32)),
-        in_specs=[whole(pltpu.SMEM), whole(v), whole(pltpu.HBM), whole(v), whole(pltpu.HBM), whole(pltpu.HBM)],
+        in_specs=[whole(pltpu.SMEM), whole(v), whole(pltpu.HBM), whole(pltpu.HBM), whole(pltpu.HBM)],
         out_specs=[whole(v), whole(pltpu.HBM)],
         scratch_shapes=[
             v((ROWS + 8, WIDTH), f32), v((NDEV, CAP, WIDTH), f32), v((NDEV, CAP, WIDTH), bf16), v((NDEV, CAP, WIDTH), f32),
             DMA((6,)),
         ],
         name="update",
-        compiler_params=pltpu.CompilerParams(vmem_limit_bytes=24 << 20),
-    )(ids, ext, rows_exp, same, base.reshape(ZB, CX * CY, WIDTH), arrived)
+        compiler_params=pltpu.CompilerParams(vmem_limit_bytes=62 << 20),
+    )(ids, ext, rows_exp, base.reshape(ZB, CX * CY, WIDTH), arrived)
 
 
 def on_device(log_density, weights, observed, inverse_var, star_counts, block_ids):
     ids, inv, pos = bucket(block_ids.T)
-    ext, ids, rows_exp, same, base, arrived = step(
+    ext, ids, rows_exp, base, arrived = step(
         ids, inv, pos, log_density, weights, star_counts, observed.T, inverse_var.T
     )
-    ext, new = update(ids, ext, rows_exp, same, base, arrived)
+    ext, new = update(ids, ext, rows_exp, base, arrived)
     return (new, ext.T)
 
 

time: 93.7 us -> 100 us (1.067)
  Pallas kernels: 84.7 us -> 99.4 us
  local copies, waits for them, and re-layouts: 7.78 us -> 0 us
    pallas_call x1, Pallas kernels: 66.9 us -> 84.2 us  [step(): pl.pallas_call(step_kernel, out_shape=(shape((STARS, BLOCKS), f32), shape...]
    unnamed x12 -> x0, local copies, waits for them, and re-layouts: 7.78 us -> none
    pallas_call x1, Pallas kernels: 15.6 us -> 13 us  [update(): pl.pallas_call(update_kernel, out_shape=(jax.ShapeDtypeStruct((STARS, BLO...]
where the time goes in v3:
time: 100 us
  Pallas kernels  99.4 us (99%)
    pallas_call x1, Pallas kernels, step(): pl.pallas_call(step_kernel, out_shape=(shape((STARS, BLOCKS), f32), shape...  84.2 us
    pallas_call x1, Pallas kernels, update(): pl.pallas_call(update_kernel, out_shape=(jax.ShapeDtypeStruct((STARS, BLO...  13 us
    pallas_call x1, Pallas kernels, bucket(): pl.pallas_call(bucket_kernel, out_shape=(shape((GX, GY, 1, CAP), i32), sh...  2.23 us

profile of v3, /device:TPU:1, one launch (start us, length us, event | category | flops | bytes accessed | tf_op | source)
XLA Modules:
  0.0 100.1 jit_solution(8794508023601471868)
XLA Ops:
  0.6 2.2 %bucket.1 = (s32[16,8,1,32]{3,2,1,0:T(1,128)}, s32[128,32]{1,0:T(8,128)}, s32[1,2048]{1,0:T(1,128)}) custom-call(s32[32,64]{1,0:T(8,128)} %bitcast.6), custom_call_target="tpu_custom_call" | custom-call | tf_op jit(solution)/shard_map/bucket/pallas_call | solution.py:84
  2.9 84.2 %step.1 = (f32[32,64]{1,0:T(8,128)}, s32[16,8,1,32]{3,2,1,0:T(1,128)}, f32[128,32,128]{2,1,0:T(8,128)}, f32[4,32,64,128]{3,2,1,0:T(8,128)}, bf16[128,32,128]{2,1,0:T(8,128)(2,1)}) custom-call(s32[16,8,1,32]{3,2,1,0:T(1,128)} %get-tuple-element.12.out_ids, s32[128,32]{1,0:T(8,128)} %get-tuple-element.13.inv_s, s32[1,2048]{1,0:T(1,128)} %get-tuple-element.14.pos_s, ...), custom_call_target="tpu_custom_call" | custom-call | tf_op jit(solution)/shard_map/step/pallas_call | solution.py:353
  87.0 13.0 %update.1 = (f32[32,64]{1,0:T(8,128)}, f32[32,64,512]{2,1,0:T(8,128)}) custom-call(s32[16,8,1,32]{3,2,1,0:T(1,128)} %get-tuple-element.15.ids, f32[32,64]{1,0:T(8,128)} %get-tuple-element.16.ext_in, f32[128,32,128]{2,1,0:T(8,128)} %get-tuple-element.17.exp_hbm, f32[4,2048,128]{2,1,0:T(8,128)} %bitcast.5, bf16[128,32,128]{2,1,0:T(8,128)(2,1)} %get-tuple-element.19.arr_hbm), custom_call_target="tpu_custom_call" | custom-call | tf_op jit(solution)/shard_map/update/pallas_call | solution.py:444

commit v4 on v3

--- a/solution.py
+++ b/solution.py
@@ -309,29 +309,28 @@
         same = jnp.where((down == across) & together, 1.0, 0.0).astype(bf16)
         parcel[at] = jnp.dot(same, stage[at].astype(bf16), preferred_element_type=f32).astype(bf16)
 
+    def partners(it):
+        return [peer(gx, gy, it * UNROLL + u + 1) for u in range(UNROLL)]
+
+    def pack_all(it):
+        for tx, ty in partners(it):
+            pack(tx, ty, tx * GY + ty)
+
+    def send_back(it, count):
+        for tx, ty in partners(it)[:count]:
+            remote(parcel.at[tx * GY + ty], arr_hbm.at[me], s_row.at[1], r_row.at[1], (tx, ty)).start()
+
     def give_back(it, _):
-        for u in range(UNROLL):
-            j = it * UNROLL + u + 1
-            tx, ty = peer(gx, gy, j)
-            at = tx * GY + ty
-            pack(tx, ty, at)
-            remote(parcel.at[at], arr_hbm.at[me], s_row.at[1], r_row.at[1], (tx, ty)).start()
+        pack_all(it)
         smooth_plane(it + 3, (it < CX - 2) | high_x)
         base_plane(it)
-        return 0
-
-    def last_trip():
-        for u in range(UNROLL):
-            j = NDEV - UNROLL + u + 1
-            tx, ty = peer(gx, gy, j)
-            at = tx * GY + ty
-            pack(tx, ty, at)
-            if u < UNROLL - 1:
-                remote(parcel.at[at], arr_hbm.at[me], s_row.at[1], r_row.at[1], (tx, ty)).start()
-        base_plane(CX - 1)
-
-    lax.fori_loop(0, NDEV // UNROLL - 1, give_back, 0)
-    last_trip()
+        send_back(it, UNROLL)
+        return 0
+
+    lax.fori_loop(0, CX - 1, give_back, 0)
+    pack_all(CX - 1)
+    send_back(CX - 1, UNROLL - 1)
+    base_plane(CX - 1)
     keep = pltpu.make_async_copy(parcel.at[me], arr_hbm.at[me], local.at[0])
     keep.start()
     base_store = pltpu.make_async_copy(base, base_hbm, local.at[2])

time: 100 us -> 80.8 us (0.81)
  Pallas kernels: 99.4 us -> 79.8 us
    pallas_call x1, Pallas kernels: 84.2 us -> 64.6 us  [step(): pl.pallas_call(step_kernel, out_shape=(shape((STARS, BLOCKS), f32), shape...]
where the time goes in v4:
time: 80.8 us; the launch traced here: 80.5 us
  Pallas kernels  79.8 us (99%)
    pallas_call x1, Pallas kernels, step(): pl.pallas_call(step_kernel, out_shape=(shape((STARS, BLOCKS), f32), shape...  64.6 us
    pallas_call x1, Pallas kernels, update(): pl.pallas_call(update_kernel, out_shape=(jax.ShapeDtypeStruct((STARS, BLO...  13 us
    pallas_call x1, Pallas kernels, bucket(): pl.pallas_call(bucket_kernel, out_shape=(shape((GX, GY, 1, CAP), i32), sh...  2.23 us

profile of v4, /device:TPU:1, one launch (start us, length us, event | category | flops | bytes accessed | tf_op | source)
XLA Modules:
  0.0 80.5 jit_solution(15836281084989737118)
XLA Ops:
  0.6 2.2 %bucket.1 = (s32[16,8,1,32]{3,2,1,0:T(1,128)}, s32[128,32]{1,0:T(8,128)}, s32[1,2048]{1,0:T(1,128)}) custom-call(s32[32,64]{1,0:T(8,128)} %bitcast.6), custom_call_target="tpu_custom_call" | custom-call | tf_op jit(solution)/shard_map/bucket/pallas_call | solution.py:84
  2.9 64.6 %step.1 = (f32[32,64]{1,0:T(8,128)}, s32[16,8,1,32]{3,2,1,0:T(1,128)}, f32[128,32,128]{2,1,0:T(8,128)}, f32[4,32,64,128]{3,2,1,0:T(8,128)}, bf16[128,32,128]{2,1,0:T(8,128)(2,1)}) custom-call(s32[16,8,1,32]{3,2,1,0:T(1,128)} %get-tuple-element.12.out_ids, s32[128,32]{1,0:T(8,128)} %get-tuple-element.13.inv_s, s32[1,2048]{1,0:T(1,128)} %get-tuple-element.14.pos_s, ...), custom_call_target="tpu_custom_call" | custom-call | tf_op jit(solution)/shard_map/step/pallas_call | solution.py:352
  67.5 13.0 %update.1 = (f32[32,64]{1,0:T(8,128)}, f32[32,64,512]{2,1,0:T(8,128)}) custom-call(s32[16,8,1,32]{3,2,1,0:T(1,128)} %get-tuple-element.15.ids, f32[32,64]{1,0:T(8,128)} %get-tuple-element.16.ext_in, f32[128,32,128]{2,1,0:T(8,128)} %get-tuple-element.17.exp_hbm, f32[4,2048,128]{2,1,0:T(8,128)} %bitcast.5, bf16[128,32,128]{2,1,0:T(8,128)(2,1)} %get-tuple-element.19.arr_hbm), custom_call_target="tpu_custom_call" | custom-call | tf_op jit(solution)/shard_map/update/pallas_call | solution.py:443

commit v5 on v4

--- a/solution.py
+++ b/solution.py
@@ -37,16 +37,53 @@
     pltpu.make_async_copy(ref, ref, sem).wait()
 
 
-def peer(gx, gy, j):
-    o = lax.rem(j * 37, NDEV)
-    x = lax.rem(gx // 4 + o // 32, 4)
-    y = lax.rem(gx + lax.rem(o // 8, 4), 4)
-    z = lax.rem(gy // 2 + lax.rem(o // 2, 4), 4)
-    c = lax.rem(gy + o, 2)
-    return x * 4 + y, z * 2 + c
-
-
-def bucket_kernel(blocks, out_ids, inv_ref, pos_ref, at_ref, bt_ref):
+def send_order():
+    dist = lambda o: sum(min(v, 4 - v) for v in o[:3])
+    rest = [(a, b, c, d) for a in range(4) for b in range(4) for c in range(4) for d in range(2)][1:]
+    rest = [rest[j * 37 % len(rest)] for j in range(len(rest))]
+    load, order = [0] * 6, []
+
+    def loaded(o):
+        now = list(load)
+        for axis in range(3):
+            now[2 * axis] += o[axis] in (1, 2)
+            now[2 * axis + 1] += o[axis] in (3, 2)
+        return now
+
+    while rest:
+        far = max(map(dist, rest))
+        spread = lambda o: (max(loaded(o)) - min(loaded(o)), sum(v * v for v in loaded(o)))
+        best = min((o for o in rest if dist(o) == far), key=spread)
+        load = loaded(best)
+        rest.remove(best)
+        order.append(best)
+    return [((a * 4 + b) * 4 + c) * 2 + d for a, b, c, d in order] + [0]
+
+
+def packed_order():
+    order = send_order()
+    return [sum(order[n + u] * NDEV ** u for u in range(UNROLL)) for n in range(0, NDEV, UNROLL)]
+
+
+def pick(words, at, first=0):
+    if len(words) == 1:
+        return jnp.int32(words[0])
+    half = len(words) // 2
+    return jnp.where(at < first + half, pick(words[:half], at, first), pick(words[half:], at, first + half))
+
+
+def partners(gx, gy, trip):
+    word, found = pick(packed_order(), trip), []
+    for u in range(UNROLL):
+        o = lax.rem(word // NDEV ** u, NDEV)
+        x = lax.rem(gx // 4 + o // 32, 4)
+        y = lax.rem(gx + lax.rem(o // 8, 4), 4)
+        z = lax.rem(gy // 2 + lax.rem(o // 2, 4), 4)
+        found.append((x * 4 + y, z * 2 + lax.rem(gy + o, 2)))
+    return found
+
+
+def bucket(blocks, out_ids, inv_ref, pos_ref, at_ref, bt_ref):
     ids = jnp.concatenate([blocks[k:k + 1, :] for k in range(SLOTS)], axis=1)
     target = ids >> LOCAL_BITS
     within = ids & (ROWS - 1)
@@ -64,7 +101,7 @@
         part = at_ref[:, cut]
         prefix = jnp.dot(part, before, preferred_element_type=f32) + running
         wide = part.astype(f32)
-        rank = jnp.sum(wide * prefix, axis=0, keepdims=True).astype(i32)
+        rank = jnp.clip(jnp.sum(wide * prefix, axis=0, keepdims=True).astype(i32), 0, CAP - 1)
         running = running + jnp.sum(wide, axis=1, keepdims=True)
         hit = slot == rank
         pos_ref[:, cut] = target[:, cut] * CAP + rank
@@ -75,20 +112,9 @@
     parts = [table[:, n * CAP:(n + 1) * CAP] for n in range(5)]
     present = parts[4] > 0.5
     row = jnp.where(present, parts[0] * 128.0 + parts[1], float(ROWS)).astype(i32)
-    out_ids[...] = row.reshape(GX, GY, 1, CAP)
-    inv_ref[...] = jnp.where(present, parts[2] * 128.0 + parts[3], float(REQ)).astype(i32)
-
-
-def bucket(blocks):
-    shape, v = jax.ShapeDtypeStruct, pltpu.VMEM
-    return pl.pallas_call(
-        bucket_kernel,
-        out_shape=(shape((GX, GY, 1, CAP), i32), shape((NDEV, CAP), i32), shape((1, REQ), i32)),
-        in_specs=[whole(v)],
-        out_specs=[whole(v)] * 3,
-        scratch_shapes=[v((NDEV, REQ), bf16), v((5 * CAP, REQ), bf16)],
-        name="bucket",
-    )(blocks)
+    out_ids[...] = jnp.clip(row, 0, ROWS).reshape(GX, GY, 1, CAP)
+    source = jnp.where(present, parts[2] * 128.0 + parts[3], float(REQ)).astype(i32)
+    inv_ref[...] = jnp.clip(source, 0, REQ)
 
 
 def shifted_sum(field, x, row):
@@ -106,9 +132,9 @@
     return centers, sides
 
 
-def step_kernel(out_ids, inv_s, pos_s, dens_hbm, weights_hbm, counts, observed, inverse_var,
+def step_kernel(blocks, dens_hbm, weights_hbm, counts, observed, inverse_var,
                 ext_out, ids_out, exp_hbm, base_hbm, arr_hbm,
-                dens, mid_ids, in_ids, ids_s,
+                dens, out_ids, mid_ids, in_ids, ids_s, inv_v, inv_s, pos_v, pos_s, at_ref, bt_ref,
                 rows_exp, served, ret, rows, w_ref, obs4, inv4, ext4, wgt4, sens, stage, parcel,
                 xlo, xhi, ylo, yhi, field, smooth, base,
                 entered, s_id, r_id, s_row, r_row, local, s_halo, r_halo):
@@ -132,6 +158,11 @@
         load.start()
     w_load.start()
 
+    bucket(blocks, out_ids, inv_v, pos_v, at_ref, bt_ref)
+    to_smem = [pltpu.make_async_copy(inv_v, inv_s, local.at[5]), pltpu.make_async_copy(pos_v, pos_s, local.at[6])]
+    for copy in to_smem:
+        copy.start()
+
     pl.semaphore_wait(barrier, len(greeted))
     for t in line:
         pl.semaphore_signal(entered, inc=1, device_id=(gx, t), device_id_type=MESH)
@@ -188,15 +219,17 @@
         rows_exp[at] = step_rate * values
         served[at] = values.astype(bf16)
 
-    def send_rows(j, _):
-        tx, ty = peer(gx, gy, j)
-        at = tx * GY + ty
-        serve(tx, ty, at)
-        remote(served.at[at], ret.at[me], s_row.at[0], r_row.at[0], (tx, ty)).start()
-        return 0
-
-    lax.fori_loop(1, NDEV, send_rows, 0)
-    serve(gx, gy, me)
+    def send_rows(trip, count):
+        for u, (tx, ty) in enumerate(partners(gx, gy, trip)):
+            at = tx * GY + ty
+            serve(tx, ty, at)
+            if u < count:
+                remote(served.at[at], ret.at[me], s_row.at[0], r_row.at[0], (tx, ty)).start()
+        return 0
+
+    trips = NDEV // UNROLL
+    lax.fori_loop(0, trips - 1, lambda trip, _: send_rows(trip, UNROLL), 0)
+    send_rows(trips - 1, UNROLL - 1)
     keep = pltpu.make_async_copy(served.at[me], ret.at[me], local.at[0])
     keep.start()
     ids_out[...] = in_ids[...]
@@ -250,6 +283,8 @@
     smooth_plane(1)
     smooth_plane(2)
     w_load.wait()
+    for copy in to_smem:
+        copy.wait()
     keep.wait()
     drain(ret.at[pl.ds(0, NDEV - 1)], r_row.at[0])
 
@@ -309,27 +344,26 @@
         same = jnp.where((down == across) & together, 1.0, 0.0).astype(bf16)
         parcel[at] = jnp.dot(same, stage[at].astype(bf16), preferred_element_type=f32).astype(bf16)
 
-    def partners(it):
-        return [peer(gx, gy, it * UNROLL + u + 1) for u in range(UNROLL)]
-
-    def pack_all(it):
-        for tx, ty in partners(it):
+    def pack_all(to):
+        for tx, ty in to:
             pack(tx, ty, tx * GY + ty)
 
-    def send_back(it, count):
-        for tx, ty in partners(it)[:count]:
+    def send_back(to):
+        for tx, ty in to:
             remote(parcel.at[tx * GY + ty], arr_hbm.at[me], s_row.at[1], r_row.at[1], (tx, ty)).start()
 
     def give_back(it, _):
-        pack_all(it)
+        to = partners(gx, gy, it)
+        pack_all(to)
         smooth_plane(it + 3, (it < CX - 2) | high_x)
         base_plane(it)
-        send_back(it, UNROLL)
+        send_back(to)
         return 0
 
     lax.fori_loop(0, CX - 1, give_back, 0)
-    pack_all(CX - 1)
-    send_back(CX - 1, UNROLL - 1)
+    to = partners(gx, gy, trips - 1)
+    pack_all(to)
+    send_back(to[:UNROLL - 1])
     base_plane(CX - 1)
     keep = pltpu.make_async_copy(parcel.at[me], arr_hbm.at[me], local.at[0])
     keep.start()
@@ -346,7 +380,7 @@
     drain(arr_hbm.at[pl.ds(0, NDEV - 1)], r_row.at[1])
 
 
-def step(ids, inv, pos, dens, weights, counts, observed, inverse_var):
+def step(blocks, dens, weights, counts, observed, inverse_var):
     shape = jax.ShapeDtypeStruct
     v = pltpu.VMEM
     return pl.pallas_call(
@@ -359,13 +393,14 @@
             shape((NDEV, CAP, WIDTH), bf16),
         ),
         in_specs=[
-            whole(v), whole(pltpu.SMEM), whole(pltpu.SMEM),
-            whole(pltpu.HBM), whole(pltpu.HBM), whole(pltpu.SMEM), whole(v), whole(v),
+            whole(v), whole(pltpu.HBM), whole(pltpu.HBM), whole(pltpu.SMEM), whole(v), whole(v),
         ],
         out_specs=[whole(v), whole(v), whole(pltpu.HBM), whole(pltpu.HBM), whole(pltpu.HBM)],
         scratch_shapes=[
             v((ROWS + 8, WIDTH), f32),
-            v((GX, GY, 1, CAP), i32), v((GX, GY, 1, CAP), i32), pltpu.SMEM((GX, GY, 1, CAP), i32),
+            v((GX, GY, 1, CAP), i32), v((GX, GY, 1, CAP), i32), v((GX, GY, 1, CAP), i32), pltpu.SMEM((GX, GY, 1, CAP), i32),
+            v((NDEV, CAP), i32), pltpu.SMEM((NDEV, CAP), i32), v((1, REQ), i32), pltpu.SMEM((1, REQ), i32),
+            v((NDEV, REQ), bf16), v((5 * CAP, REQ), bf16),
             v((NDEV, CAP, WIDTH), f32), v((NDEV, CAP, WIDTH), bf16), v((NDEV, CAP, WIDTH), bf16),
             v((NDEV * CAP, WIDTH), f32), v((BLOCKS, SLOTS, STARS, WIDTH), bf16),
             v((WIDTH, WIDTH), f32), v((WIDTH, WIDTH), f32), v((BLOCKS, WIDTH), f32), v((BLOCKS, WIDTH), f32),
@@ -377,7 +412,7 @@
         ],
         name="step",
         compiler_params=pltpu.CompilerParams(collective_id=0, has_side_effects=True, vmem_limit_bytes=60 << 20),
-    )(ids, inv, pos, dens, weights, counts, observed, inverse_var)
+    )(blocks, dens, weights, counts, observed, inverse_var)
 
 
 def update_kernel(ids, ext_in, exp_hbm, base_hbm, arr_hbm, ext_out, out_hbm, new, rows_exp, arrived, add, sem):
@@ -455,9 +490,8 @@
 
 
 def on_device(log_density, weights, observed, inverse_var, star_counts, block_ids):
-    ids, inv, pos = bucket(block_ids.T)
     ext, ids, rows_exp, base, arrived = step(
-        ids, inv, pos, log_density, weights, star_counts, observed.T, inverse_var.T
+        block_ids.T, log_density, weights, star_counts, observed.T, inverse_var.T
     )
     ext, new = update(ids, ext, rows_exp, base, arrived)
     return (new, ext.T)

time: 80.8 us -> 75.9 us (0.939)
  Pallas kernels: 79.8 us -> 75 us
    pallas_call x1, Pallas kernels: 64.6 us -> 61.9 us  [step(): pl.pallas_call(step_kernel, out_shape=(shape((STARS, BLOCKS), f32), shape...]
    pallas_call x1 -> x0, Pallas kernels: 2.23 us -> none  [bucket(): pl.pallas_call(bucket_kernel, out_shape=(shape((GX, GY, 1, CAP), i32), sh...]
where the time goes in v5:
time: 75.9 us; the launch traced here: 75.6 us
  Pallas kernels  75 us (99%)
    pallas_call x1, Pallas kernels, step(): pl.pallas_call(step_kernel, out_shape=(shape((STARS, BLOCKS), f32), shape...  61.9 us
    pallas_call x1, Pallas kernels, update(): pl.pallas_call(update_kernel, out_shape=(jax.ShapeDtypeStruct((STARS, BLO...  13.1 us

profile of v5, /device:TPU:1, one launch (start us, length us, event | category | flops | bytes accessed | tf_op | source)
XLA Modules:
  0.0 75.6 jit_solution(6020513871900468033)
XLA Ops:
  0.6 61.9 %step.1 = (f32[32,64]{1,0:T(8,128)}, s32[16,8,1,32]{3,2,1,0:T(1,128)}, f32[128,32,128]{2,1,0:T(8,128)}, f32[4,32,64,128]{3,2,1,0:T(8,128)}, bf16[128,32,128]{2,1,0:T(8,128)(2,1)}) custom-call(s32[32,64]{1,0:T(8,128)} %bitcast.6, f32[32,64,512]{2,1,0:T(8,128)} %dens_hbm.1, bf16[64,32,32,128]{3,2,1,0:T(8,128)(2,1)} %weights_hbm.1, s32[64]{0:T(128)} %counts.1, ...), custom_call_target="tpu_custom_call" | custom-call | tf_op jit(solution)/shard_map/step/pallas_call | solution.py:386
  62.5 13.1 %update.1 = (f32[32,64]{1,0:T(8,128)}, f32[32,64,512]{2,1,0:T(8,128)}) custom-call(s32[16,8,1,32]{3,2,1,0:T(1,128)} %get-tuple-element.9.ids, f32[32,64]{1,0:T(8,128)} %get-tuple-element.10.ext_in, f32[128,32,128]{2,1,0:T(8,128)} %get-tuple-element.11.exp_hbm, f32[4,2048,128]{2,1,0:T(8,128)} %bitcast.5, bf16[128,32,128]{2,1,0:T(8,128)(2,1)} %get-tuple-element.13.arr_hbm), custom_call_target="tpu_custom_call" | custom-call | tf_op jit(solution)/shard_map/update/pallas_call | solution.py:478

commit v6 on v5

--- a/solution.py
+++ b/solution.py
@@ -132,8 +132,9 @@
     return centers, sides
 
 
-def step_kernel(blocks, dens_hbm, weights_hbm, counts, observed, inverse_var,
-                ext_out, ids_out, exp_hbm, base_hbm, arr_hbm,
+def step_kernel(blocks, dens_hbm, weights_hbm, counts_hbm, observed_hbm, inverse_hbm,
+                ext_hbm, ids_hbm, exp_hbm, base_hbm, arr_hbm,
+                counts, observed, inverse_var, ext_t,
                 dens, out_ids, mid_ids, in_ids, ids_s, inv_v, inv_s, pos_v, pos_s, at_ref, bt_ref,
                 rows_exp, served, ret, rows, w_ref, obs4, inv4, ext4, wgt4, sens, stage, parcel,
                 xlo, xhi, ylo, yhi, field, smooth, base,
@@ -157,6 +158,12 @@
     for load in loads:
         load.start()
     w_load.start()
+    small = [
+        pltpu.make_async_copy(src, dst, local.at[8 + n])
+        for n, (src, dst) in enumerate(((counts_hbm, counts), (observed_hbm, observed), (inverse_hbm, inverse_var)))
+    ]
+    for load in small:
+        load.start()
 
     bucket(blocks, out_ids, inv_v, pos_v, at_ref, bt_ref)
     to_smem = [pltpu.make_async_copy(inv_v, inv_s, local.at[5]), pltpu.make_async_copy(pos_v, pos_s, local.at[6])]
@@ -202,6 +209,8 @@
     for copy in halos:
         copy.start()
 
+    for load in small:
+        load.wait()
     for ref, four in ((observed, obs4), (inverse_var, inv4)):
         wide = jnp.concatenate([ref[...], ref[...]], axis=1)
         four[...] = jnp.concatenate([wide] * 4, axis=0).T
@@ -210,6 +219,8 @@
     drain(in_ids.at[:, pl.ds(0, GY - 1)], r_id.at[1])
     ids_copy = pltpu.make_async_copy(in_ids, ids_s, local.at[7])
     ids_copy.start()
+    ids_store = pltpu.make_async_copy(in_ids, ids_hbm, local.at[11])
+    ids_store.start()
     ids_copy.wait()
 
     def serve(tx, ty, at):
@@ -232,7 +243,6 @@
     send_rows(trips - 1, UNROLL - 1)
     keep = pltpu.make_async_copy(served.at[me], ret.at[me], local.at[0])
     keep.start()
-    ids_out[...] = in_ids[...]
     exp_store = pltpu.make_async_copy(rows_exp, exp_hbm, local.at[1])
     exp_store.start()
 
@@ -280,8 +290,13 @@
                 base[q, x, pl.ds(8 * n, 8), :] = now - (step_rate * prior_weight) * prior
 
     smooth_plane(0, low_x)
-    smooth_plane(1)
-    smooth_plane(2)
+
+    def smooth_all(x, _):
+        smooth_plane(x)
+        return 0
+
+    lax.fori_loop(1, CX + 1, smooth_all, 0)
+    smooth_plane(CX + 1, high_x)
     w_load.wait()
     for copy in to_smem:
         copy.wait()
@@ -332,6 +347,9 @@
 
     lax.fori_loop(1, BLOCKS // UNROLL, both, 0)
     sensitive(BLOCKS // UNROLL - 1)
+    ext_t[...] = jnp.concatenate([ext4[...], ext4[...]], axis=0).T[:STARS, :BLOCKS]
+    ext_store = pltpu.make_async_copy(ext_t, ext_hbm, local.at[12])
+    ext_store.start()
 
     slot_a, slot_b = lax.broadcasted_iota(i32, (CAP, CAP), 0), lax.broadcasted_iota(i32, (CAP, CAP), 1)
     eye, together = slot_a == slot_b, (slot_a >> 3) == (slot_b >> 3)
@@ -355,7 +373,6 @@
     def give_back(it, _):
         to = partners(gx, gy, it)
         pack_all(to)
-        smooth_plane(it + 3, (it < CX - 2) | high_x)
         base_plane(it)
         send_back(to)
         return 0
@@ -369,8 +386,9 @@
     keep.start()
     base_store = pltpu.make_async_copy(base, base_hbm, local.at[2])
     base_store.start()
-    ext_out[...] = jnp.concatenate([ext4[...], ext4[...]], axis=0).T[:STARS, :BLOCKS]
     keep.wait()
+    ids_store.wait()
+    ext_store.wait()
     exp_store.wait()
     base_store.wait()
     drain(out_ids.at[pl.ds(0, GX - 1)], s_id.at[0])
@@ -393,10 +411,11 @@
             shape((NDEV, CAP, WIDTH), bf16),
         ),
         in_specs=[
-            whole(v), whole(pltpu.HBM), whole(pltpu.HBM), whole(pltpu.SMEM), whole(v), whole(v),
+            whole(v), whole(pltpu.HBM), whole(pltpu.HBM), whole(pltpu.HBM), whole(pltpu.HBM), whole(pltpu.HBM),
         ],
-        out_specs=[whole(v), whole(v), whole(pltpu.HBM), whole(pltpu.HBM), whole(pltpu.HBM)],
+        out_specs=[whole(pltpu.HBM)] * 5,
         scratch_shapes=[
+            pltpu.SMEM((BLOCKS,), i32), v((STARS, BLOCKS), f32), v((STARS, BLOCKS), f32), v((STARS, BLOCKS), f32),
             v((ROWS + 8, WIDTH), f32),
             v((GX, GY, 1, CAP), i32), v((GX, GY, 1, CAP), i32), v((GX, GY, 1, CAP), i32), pltpu.SMEM((GX, GY, 1, CAP), i32),
             v((NDEV, CAP), i32), pltpu.SMEM((NDEV, CAP), i32), v((1, REQ), i32), pltpu.SMEM((1, REQ), i32),
@@ -408,23 +427,26 @@
             v((ZB, 2, CY, WIDTH), f32), v((ZB, 2, CY, WIDTH), f32),
             v((ZB, CX + 2, 8, WIDTH), f32), v((ZB, CX + 2, 8, WIDTH), f32),
             v((ZB, CX + 4, CY + 16, WIDTH), f32), v((ZB, CX + 2, CY + 8, WIDTH), f32), v((ZB, CX, CY, WIDTH), f32),
-            pltpu.SemaphoreType.REGULAR, DMA((2,)), DMA((2,)), DMA((2,)), DMA((2,)), DMA((8,)), DMA((8,)), DMA((8,)),
+            pltpu.SemaphoreType.REGULAR, DMA((2,)), DMA((2,)), DMA((2,)), DMA((2,)), DMA((13,)), DMA((8,)), DMA((8,)),
         ],
         name="step",
         compiler_params=pltpu.CompilerParams(collective_id=0, has_side_effects=True, vmem_limit_bytes=60 << 20),
     )(blocks, dens, weights, counts, observed, inverse_var)
 
 
-def update_kernel(ids, ext_in, exp_hbm, base_hbm, arr_hbm, ext_out, out_hbm, new, rows_exp, arrived, add, sem):
+def update_kernel(ids_hbm, ext_in, exp_hbm, base_hbm, arr_hbm, ext_out, out_hbm, ids, new, rows_exp, arrived, add, sem):
     load_exp = pltpu.make_async_copy(exp_hbm, rows_exp, sem.at[0])
     load_arr = pltpu.make_async_copy(arr_hbm, arrived, sem.at[1])
     load_exp.start()
     load_arr.start()
+    load_ids = pltpu.make_async_copy(ids_hbm, ids, sem.at[6])
+    load_ids.start()
     bases = []
     for q in range(ZB):
         bases.append(pltpu.make_async_copy(base_hbm.at[q], new.at[pl.ds(q * CX * CY, CX * CY)], sem.at[2 + q]))
         bases[q].start()
-    ext_out[...] = ext_in[...]
+    ext_copy = pltpu.make_async_copy(ext_in, ext_out, sem.at[7])
+    ext_copy.start()
     new[pl.ds(ROWS, 8), :] = jnp.zeros((8, WIDTH), f32)
     load_exp.wait()
     load_arr.wait()
@@ -436,6 +458,7 @@
         return 0
 
     lax.fori_loop(0, NDEV // UNROLL, scale, 0)
+    load_ids.wait()
     for load in bases:
         load.wait()
 
@@ -469,6 +492,7 @@
             rows_of.reshape(CX, CY, WIDTH), out_hbm.at[:, :, pl.ds(q * WIDTH, WIDTH)], sem.at[2 + q]
         ))
         stores[q].start()
+    ext_copy.wait()
     for store in stores:
         store.wait()
 
@@ -478,11 +502,12 @@
     return pl.pallas_call(
         update_kernel,
         out_shape=(jax.ShapeDtypeStruct((STARS, BLOCKS), f32), jax.ShapeDtypeStruct((CX, CY, ZB * WIDTH), f32)),
-        in_specs=[whole(pltpu.SMEM), whole(v), whole(pltpu.HBM), whole(pltpu.HBM), whole(pltpu.HBM)],
-        out_specs=[whole(v), whole(pltpu.HBM)],
+        in_specs=[whole(pltpu.HBM)] * 5,
+        out_specs=[whole(pltpu.HBM)] * 2,
         scratch_shapes=[
+            pltpu.SMEM((GX, GY, 1, CAP), i32),
             v((ROWS + 8, WIDTH), f32), v((NDEV, CAP, WIDTH), f32), v((NDEV, CAP, WIDTH), bf16), v((NDEV, CAP, WIDTH), f32),
-            DMA((6,)),
+            DMA((8,)),
         ],
         name="update",
         compiler_params=pltpu.CompilerParams(vmem_limit_bytes=62 << 20),

time: 75.9 us -> 73.7 us (0.971)
  Pallas kernels: 75 us -> 72.8 us
    pallas_call x1, Pallas kernels: 13.1 us -> 10.8 us  [update(): pl.pallas_call(update_kernel, out_shape=(jax.ShapeDtypeStruct((STARS, BLO...]
where the time goes in v6:
time: 73.7 us; the launch traced here: 73.4 us
  Pallas kernels  72.8 us (99%)
    pallas_call x1, Pallas kernels, step(): pl.pallas_call(step_kernel, out_shape=(shape((STARS, BLOCKS), f32), shape...  62 us
    pallas_call x1, Pallas kernels, update(): pl.pallas_call(update_kernel, out_shape=(jax.ShapeDtypeStruct((STARS, BLO...  10.8 us

profile of v6, /device:TPU:1, one launch (start us, length us, event | category | flops | bytes accessed | tf_op | source)
XLA Modules:
  0.0 73.4 jit_solution(10893661738126958542)
XLA Ops:
  0.6 62.0 %step.1 = (f32[32,64]{1,0:T(8,128)}, s32[16,8,1,32]{3,2,1,0:T(1,128)}, f32[128,32,128]{2,1,0:T(8,128)}, f32[4,32,64,128]{3,2,1,0:T(8,128)}, bf16[128,32,128]{2,1,0:T(8,128)(2,1)}) custom-call(s32[32,64]{1,0:T(8,128)} %bitcast.6, f32[32,64,512]{2,1,0:T(8,128)} %dens_hbm.1, bf16[64,32,32,128]{3,2,1,0:T(8,128)(2,1)} %weights_hbm.1, s32[64]{0:T(128)} %counts_hbm.1, ...), custom_call_target="tpu_custom_call" | custom-call | tf_op jit(solution)/shard_map/step/pallas_call | solution.py:404
  62.6 10.8 %update.1 = (f32[32,64]{1,0:T(8,128)}, f32[32,64,512]{2,1,0:T(8,128)}) custom-call(s32[16,8,1,32]{3,2,1,0:T(1,128)} %get-tuple-element.9.ids_hbm, f32[32,64]{1,0:T(8,128)} %get-tuple-element.10.ext_in, f32[128,32,128]{2,1,0:T(8,128)} %get-tuple-element.11.exp_hbm, f32[4,2048,128]{2,1,0:T(8,128)} %bitcast.5, bf16[128,32,128]{2,1,0:T(8,128)(2,1)} %get-tuple-element.13.arr_hbm), custom_call_target="tpu_custom_call" | custom-call | tf_op jit(solution)/shard_map/update/pallas_call | solution.py:502

commit v7 on v6

--- a/solution.py
+++ b/solution.py
@@ -183,14 +183,16 @@
     halos = [
         (field.at[:, pl.ds(CX, 2), pl.ds(8, CY)], xlo, (gxp, gy)),
         (field.at[:, pl.ds(2, 2), pl.ds(8, CY)], xhi, (gxm, gy)),
-        (field.at[:, pl.ds(2, CX), pl.ds(CY, 8)], ylo.at[:, pl.ds(1, CX)], (gx, gyp)),
-        (field.at[:, pl.ds(2, CX), pl.ds(8, 8)], yhi.at[:, pl.ds(1, CX)], (gx, gym)),
+        (field.at[:, pl.ds(2, CX), pl.ds(CY + 6, 2)], ylo.at[:, pl.ds(1, CX), pl.ds(6, 2)], (gx, gyp)),
+        (field.at[:, pl.ds(2, CX), pl.ds(8, 2)], yhi.at[:, pl.ds(1, CX), pl.ds(0, 2)], (gx, gym)),
         (field.at[:, CX + 1, pl.ds(CY, 8)], ylo.at[:, 0], (gxp, gyp)),
         (field.at[:, 2, pl.ds(CY, 8)], ylo.at[:, CX + 1], (gxm, gyp)),
         (field.at[:, CX + 1, pl.ds(8, 8)], yhi.at[:, 0], (gxp, gym)),
         (field.at[:, 2, pl.ds(8, 8)], yhi.at[:, CX + 1], (gxm, gym)),
     ]
     halos = [remote(src, dst, s_halo.at[n], r_halo.at[n], to) for n, (src, dst, to) in enumerate(halos)]
+    for copy in halos:
+        copy.start()
 
     def gather_source(x, _):
         for q in range(ZB):
@@ -206,8 +208,6 @@
     own.start()
     for t in line:
         remote(mid_ids.at[:, t], in_ids.at[:, gy], s_id.at[1], r_id.at[1], (gx, t)).start()
-    for copy in halos:
-        copy.start()
 
     for load in small:
         load.wait()
@@ -484,7 +484,7 @@
 
         return 0
 
-    lax.fori_loop(0, NDEV, source, 0)
+    lax.fori_loop(0, NDEV, source, 0, unroll=2)
     stores = []
     for q in range(ZB):
         rows_of = new.at[pl.ds(q * CX * CY, CX * CY)]

time: 73.7 us -> 71.9 us (0.976)
  Pallas kernels: 72.8 us -> 71 us
    pallas_call x1, Pallas kernels: 62 us -> 60.7 us  [step(): pl.pallas_call(step_kernel, out_shape=(shape((STARS, BLOCKS), f32), shape...]
where the time goes in v7:
time: 71.9 us; the launch traced here: 71.6 us
  Pallas kernels  71 us (99%)
    pallas_call x1, Pallas kernels, step(): pl.pallas_call(step_kernel, out_shape=(shape((STARS, BLOCKS), f32), shape...  60.7 us
    pallas_call x1, Pallas kernels, update(): pl.pallas_call(update_kernel, out_shape=(jax.ShapeDtypeStruct((STARS, BLO...  10.3 us

profile of v7, /device:TPU:1, one launch (start us, length us, event | category | flops | bytes accessed | tf_op | source)
XLA Modules:
  0.0 71.6 jit_solution(7650296796038332100)
XLA Ops:
  0.6 60.7 %step.1 = (f32[32,64]{1,0:T(8,128)}, s32[16,8,1,32]{3,2,1,0:T(1,128)}, f32[128,32,128]{2,1,0:T(8,128)}, f32[4,32,64,128]{3,2,1,0:T(8,128)}, bf16[128,32,128]{2,1,0:T(8,128)(2,1)}) custom-call(s32[32,64]{1,0:T(8,128)} %bitcast.6, f32[32,64,512]{2,1,0:T(8,128)} %dens_hbm.1, bf16[64,32,32,128]{3,2,1,0:T(8,128)(2,1)} %weights_hbm.1, s32[64]{0:T(128)} %counts_hbm.1, ...), custom_call_target="tpu_custom_call" | custom-call | tf_op jit(solution)/shard_map/step/pallas_call | solution.py:404
  61.3 10.3 %update.1 = (f32[32,64]{1,0:T(8,128)}, f32[32,64,512]{2,1,0:T(8,128)}) custom-call(s32[16,8,1,32]{3,2,1,0:T(1,128)} %get-tuple-element.9.ids_hbm, f32[32,64]{1,0:T(8,128)} %get-tuple-element.10.ext_in, f32[128,32,128]{2,1,0:T(8,128)} %get-tuple-element.11.exp_hbm, f32[4,2048,128]{2,1,0:T(8,128)} %bitcast.5, bf16[128,32,128]{2,1,0:T(8,128)(2,1)} %get-tuple-element.13.arr_hbm), custom_call_target="tpu_custom_call" | custom-call | tf_op jit(solution)/shard_map/update/pallas_call | solution.py:502

commit v8 on v7

--- a/solution.py
+++ b/solution.py
@@ -20,6 +20,7 @@
 ROWS = CX * CY * ZB
 LOCAL_BITS = 13
 UNROLL = 4
+STAR_UNROLL = 8
 center_weight = shift_kappa + 6.0
 
 
@@ -231,11 +232,11 @@
         served[at] = values.astype(bf16)
 
     def send_rows(trip, count):
-        for u, (tx, ty) in enumerate(partners(gx, gy, trip)):
-            at = tx * GY + ty
-            serve(tx, ty, at)
-            if u < count:
-                remote(served.at[at], ret.at[me], s_row.at[0], r_row.at[0], (tx, ty)).start()
+        to = partners(gx, gy, trip)
+        for tx, ty in to:
+            serve(tx, ty, tx * GY + ty)
+        for tx, ty in to[:count]:
+            remote(served.at[tx * GY + ty], ret.at[me], s_row.at[0], r_row.at[0], (tx, ty)).start()
         return 0
 
     trips = NDEV // UNROLL
@@ -316,8 +317,8 @@
     star = lax.broadcasted_iota(i32, (1, WIDTH), 1) & (STARS - 1)
 
     def extinct(i):
-        for u in range(UNROLL):
-            b = i * UNROLL + u
+        for u in range(STAR_UNROLL):
+            b = i * STAR_UNROLL + u
             totals = [jnp.zeros((STARS, WIDTH), f32) for _ in range(2)]
             for k in range(SLOTS):
                 line_k = rows[pl.ds(pos_s[0, k * BLOCKS + b], 1), :]
@@ -329,8 +330,8 @@
             wgt4[pl.ds(b, 1), :] = jnp.where(star < counts[b], residual, 0.0)
 
     def sensitive(i):
-        for u in range(UNROLL):
-            b = i * UNROLL + u
+        for u in range(STAR_UNROLL):
+            b = i * STAR_UNROLL + u
             line_b = wgt4[pl.ds(b, 1), :]
             left = jnp.where(mine, jnp.concatenate([line_b, line_b], axis=1), 0.0).astype(bf16)
             for n in range(SLOTS // 8):
@@ -345,8 +346,8 @@
         extinct(i)
         return 0
 
-    lax.fori_loop(1, BLOCKS // UNROLL, both, 0)
-    sensitive(BLOCKS // UNROLL - 1)
+    lax.fori_loop(1, BLOCKS // STAR_UNROLL, both, 0)
+    sensitive(BLOCKS // STAR_UNROLL - 1)
     ext_t[...] = jnp.concatenate([ext4[...], ext4[...]], axis=0).T[:STARS, :BLOCKS]
     ext_store = pltpu.make_async_copy(ext_t, ext_hbm, local.at[12])
     ext_store.start()

time: 71.9 us -> 71.4 us (level)
  no operation moved by 1% of the time
where the time goes in v8:
time: 71.4 us; the launch traced here: 71.2 us
  Pallas kernels  70.5 us (99%)
    pallas_call x1, Pallas kernels, step(): pl.pallas_call(step_kernel, out_shape=(shape((STARS, BLOCKS), f32), shape...  60.1 us
    pallas_call x1, Pallas kernels, update(): pl.pallas_call(update_kernel, out_shape=(jax.ShapeDtypeStruct((STARS, BLO...  10.5 us

profile of v8, /device:TPU:1, one launch (start us, length us, event | category | flops | bytes accessed | tf_op | source)
XLA Modules:
  0.0 71.2 jit_solution(6013440026515664712)
XLA Ops:
  0.6 60.1 %step.1 = (f32[32,64]{1,0:T(8,128)}, s32[16,8,1,32]{3,2,1,0:T(1,128)}, f32[128,32,128]{2,1,0:T(8,128)}, f32[4,32,64,128]{3,2,1,0:T(8,128)}, bf16[128,32,128]{2,1,0:T(8,128)(2,1)}) custom-call(s32[32,64]{1,0:T(8,128)} %bitcast.6, f32[32,64,512]{2,1,0:T(8,128)} %dens_hbm.1, bf16[64,32,32,128]{3,2,1,0:T(8,128)(2,1)} %weights_hbm.1, s32[64]{0:T(128)} %counts_hbm.1, ...), custom_call_target="tpu_custom_call" | custom-call | tf_op jit(solution)/shard_map/step/pallas_call | solution.py:405
  60.7 10.5 %update.1 = (f32[32,64]{1,0:T(8,128)}, f32[32,64,512]{2,1,0:T(8,128)}) custom-call(s32[16,8,1,32]{3,2,1,0:T(1,128)} %get-tuple-element.9.ids_hbm, f32[32,64]{1,0:T(8,128)} %get-tuple-element.10.ext_in, f32[128,32,128]{2,1,0:T(8,128)} %get-tuple-element.11.exp_hbm, f32[4,2048,128]{2,1,0:T(8,128)} %bitcast.5, bf16[128,32,128]{2,1,0:T(8,128)(2,1)} %get-tuple-element.13.arr_hbm), custom_call_target="tpu_custom_call" | custom-call | tf_op jit(solution)/shard_map/update/pallas_call | solution.py:503
